TPU v7x, 256 devices: a whole 4x4x8 slice. The times are simulated.
256 devices in a mesh: frames: 8 (over x, core), rows: 32 (over y, z).
Axes of the slice: x: 4, y: 4, z: 8, core: 2. Of those that a mesh axis runs over, the one named last changes fastest.
Arguments:
- observed: float32 [32, 2048, 2048], P('frames', 'rows'), may hold values from 0.25 to 4
- kernel: float32 [2048, 65], P('rows'), may hold values from 0.004 to 0.04
- row_shift: int32 [2048], P('rows'), may hold values from -8 to 8
- cycle_map: float32 [2048, 256], P('rows'), may hold values from 0 to 0.03125
- cycle_blocks: int32 [32, 8], P('rows'), may hold values from 0 to 63
- chi_map: bfloat16 [32, 2048, 720], P('rows'), may hold values from 0 to 3.0517578e-05
Outputs:
- binned: float32 [2048, 720], P('rows')
All inputs are finite; a program needn't handle non-finite values.
Results may differ from a plain program's by a relative error of at most 0.0003.
Values sent between devices are 32-bit elements; how exact they have to be, the bound alone decides.
A program may use at most 128 MiB of HBM per device.

v0:
```python
import jax
import jax.numpy as jnp
from jax import lax
from jax.sharding import PartitionSpec as P

SHIFT = 8
ITERS = 4
Q = 2048
CHI = 720
QB = 32
NB = 8


def shifted(block, axis, distance):
    devices = range(lax.axis_size(axis))
    route = [(i - distance, i) for i in devices if i - distance in devices]
    return lax.ppermute(block, axis, route)


def extended(cells, sides, width):
    for axis, dim in sides:
        count = lax.axis_size(axis)
        ends = count - 1
        head = lax.slice_in_dim(cells, 0, width, axis=dim)
        tail = lax.slice_in_dim(cells, cells.shape[dim] - width, cells.shape[dim], axis=dim)
        cells = jnp.concatenate(
            [
                lax.ppermute(tail, axis, [(i, (i + 1) % count) for i in range(ends)]),
                cells,
                lax.ppermute(head, axis, [((i + 1) % count, i) for i in range(ends)]),
            ],
            axis=dim,
        )
    return cells


def band_matrix(kernel, row_shift, first_row, total_rows, halo_rows):
    rows_here = kernel.shape[0]
    band_width = kernel.shape[1]
    half_band = (band_width - 1) // 2
    local_rows = jnp.arange(rows_here, dtype=jnp.int32)[:, None]
    tap_index = jnp.arange(band_width, dtype=jnp.int32)[None, :]
    target = local_rows + row_shift[:, None] + tap_index - half_band
    global_rows = target + first_row
    inside = (global_rows >= 0) & (global_rows < total_rows)
    weights = jnp.where(inside, kernel, jnp.float32(0.0))
    columns = jnp.arange(rows_here + 2 * halo_rows, dtype=jnp.int32)
    matches = (target[:, :, None] + halo_rows == columns[None, None, :]).astype(jnp.float32)
    return jnp.einsum("ik,ikj->ij", weights, matches, precision=lax.Precision.HIGHEST)


def rim_tables(rows_here, halo_rows):
    top_place = jnp.eye(halo_rows, rows_here, dtype=jnp.float32)
    bottom_place = jnp.eye(halo_rows, rows_here, k=rows_here - halo_rows, dtype=jnp.float32)
    return (top_place, bottom_place)


def body(observed, kernel, row_shift, cycle_map, cycle_blocks, chi_map):
    rows_here = observed.shape[1]
    tile_count = lax.axis_size("rows")
    first_row = lax.axis_index("rows") * rows_here
    halo_rows = (kernel.shape[1] - 1) // 2 + SHIFT
    band_mat = band_matrix(kernel, row_shift, first_row, rows_here * tile_count, halo_rows)
    top_place, bottom_place = rim_tables(rows_here, halo_rows)
    upper_band = band_mat[:, :halo_rows]
    centre_band = band_mat[:, halo_rows : halo_rows + rows_here]
    lower_band = band_mat[:, halo_rows + rows_here :]

    def spread(upper_rim, centre, lower_rim):
        from_below = shifted(upper_rim, "rows", -1)
        from_above = shifted(lower_rim, "rows", 1)
        centre = centre + jnp.einsum(
            "hr,fhc->frc", top_place, from_above, precision=lax.Precision.HIGHEST
        )
        return centre + jnp.einsum(
            "hr,fhc->frc", bottom_place, from_below, precision=lax.Precision.HIGHEST
        )

    norm_sums = spread(
        jnp.sum(upper_band, axis=0)[None, :, None],
        jnp.sum(centre_band, axis=0)[None, :, None],
        jnp.sum(lower_band, axis=0)[None, :, None],
    )
    estimate = observed
    for repeat in range(ITERS):
        padded = extended(estimate, (("rows", 1),), halo_rows)
        blurred = jnp.einsum("ij,fjc->fic", band_mat, padded, precision=lax.Precision.HIGHEST)
        ratios = observed / blurred
        upper_part = jnp.einsum("ij,fic->fjc", upper_band, ratios, precision=lax.Precision.HIGHEST)
        centre_part = jnp.einsum(
            "ij,fic->fjc", centre_band, ratios, precision=lax.Precision.HIGHEST
        )
        lower_part = jnp.einsum("ij,fic->fjc", lower_band, ratios, precision=lax.Precision.HIGHEST)
        backed = spread(upper_part, centre_part, lower_part)
        estimate = estimate * backed / norm_sums
    summed = jnp.sum(estimate, axis=0)
    cycle_part = jnp.einsum("rq,rc->qc", cycle_map, summed, precision=lax.Precision.HIGHEST).astype(
        jnp.bfloat16
    )
    blocks = jnp.dot(cycle_part, chi_map[0], preferred_element_type=jnp.float32).reshape(
        NB, QB, CHI
    )
    onehot = (jnp.arange(Q // QB, dtype=jnp.int32)[:, None] == cycle_blocks[0][None, :]).astype(
        jnp.float32
    )
    owned = lax.psum_scatter(
        jnp.einsum("kb,bqc->kqc", onehot, blocks, precision=lax.Precision.HIGHEST).reshape(Q, CHI),
        "rows",
        scatter_dimension=0,
        tiled=True,
    )
    binned = lax.psum(owned, "frames")
    return binned


def solution(mesh):
    return jax.shard_map(
        body,
        mesh=mesh,
        in_specs=(
            P("frames", "rows", None),
            P("rows", None),
            P("rows"),
            P("rows", None),
            P("rows", None),
            P("rows", None, None),
        ),
        out_specs=P("rows", None),
        check_vma=False,
    )
```

profile of v0, /device:TPU:1, one launch (start us, length us, event | category | flops | bytes accessed | tf_op | source)
XLA Modules:
  0.0 627.5 jit_solution(18317069830610186839)
XLA Ops:
  6.5 3.7 fusion.137
  10.2 5.4 collective-permute-start
  19.4 22.9 %collective-permute-done = f32[4,40,2048]{2,1,0:T(8,128)} collective-permute-done((f32[4,40,2048]{2,1,0:T(8,128)}, f32[4,40,2048]{2,1,0:T(8,128)}, u32[]{:S(2)}, u32[]{:S(2)}) %collective-permute-start) | collective-permute-done | bytes 1310752 | tf_op jit(solution)/shard_map/ppermute | solution.py:28
  42.3 4.8 collective-permute-done.1
  47.2 6.2 fusion.52
  54.9 3.0 collective-permute-start.2
  62.2 6.5 %collective-permute-start.4 = (f32[1,40,1]{1,2,0:T(1,128)S(1)}, f32[1,40,1]{1,2,0:T(1,128)S(1)}, u32[]{:S(2)}, u32[]{:S(2)}) collective-permute-start(f32[1,40,1]{1,2,0:T(1,128)S(1)} %bitcast.191), channel_id=1, source_target_pairs={{0,1},{1,2},{2,3},{3,4},{4,5},{5,6},{6,7},{7,8},{8,9},{9,10},{10,1... | collective-permute-start | bytes 488 | tf_op jit(solution)/shard_map/ppermute | solution.py:17
  68.8 22.7 %collective-permute-done.5 = f32[1,40,1]{1,2,0:T(1,128)S(1)} collective-permute-done((f32[1,40,1]{1,2,0:T(1,128)S(1)}, f32[1,40,1]{1,2,0:T(1,128)S(1)}, u32[]{:S(2)}, u32[]{:S(2)}) %collective-permute-start.5) | collective-permute-done | bytes 192 | tf_op jit(solution)/shard_map/ppermute | solution.py:17
  97.5 4.0 collective-permute-start.6
  102.9 23.8 %collective-permute-done.6 = f32[4,40,2048]{2,1,0:T(8,128)S(1)} collective-permute-done((f32[4,40,2048]{2,1,0:T(8,128)S(1)}, f32[4,40,2048]{2,1,0:T(8,128)S(1)}, u32[]{:S(2)}, u32[]{:S(2)}) %collective-permute-start.6) | collective-permute-done | bytes 1310752 | tf_op jit(solution)/shard_map/ppermute | solution.py:28
  126.7 3.9 collective-permute-done.7
  130.6 3.1 fusion.55
  135.3 2.9 collective-permute-start.8
  143.3 18.6 %collective-permute-done.8 = f32[4,40,2048]{2,1,0:T(8,128)S(1)} collective-permute-done((f32[4,40,2048]{2,1,0:T(8,128)S(1)}, f32[4,40,2048]{2,1,0:T(8,128)S(1)}, u32[]{:S(2)}, u32[]{:S(2)}) %collective-permute-start.8) | collective-permute-done | bytes 1310752 | tf_op jit(solution)/shard_map/ppermute | solution.py:17
  163.1 4.5 collective-permute-done.9
  169.6 3.6 collective-permute-start.10
  174.5 21.4 %collective-permute-done.10 = f32[4,40,2048]{2,1,0:T(8,128)S(1)} collective-permute-done((f32[4,40,2048]{2,1,0:T(8,128)S(1)}, f32[4,40,2048]{2,1,0:T(8,128)S(1)}, u32[]{:S(2)}, u32[]{:S(2)}) %collective-permute-start.10) | collective-permute-done | bytes 1310752 | tf_op jit(solution)/shard_map/ppermute | solution.py:28
  196.0 4.2 collective-permute-done.11
  200.2 3.1 fusion.58
  204.9 3.5 collective-permute-start.12
  213.7 16.4 %collective-permute-done.12 = f32[4,40,2048]{2,1,0:T(8,128)S(1)} collective-permute-done((f32[4,40,2048]{2,1,0:T(8,128)S(1)}, f32[4,40,2048]{2,1,0:T(8,128)S(1)}, u32[]{:S(2)}, u32[]{:S(2)}) %collective-permute-start.12) | collective-permute-done | bytes 1310752 | tf_op jit(solution)/shard_map/ppermute | solution.py:17
  231.4 4.2 collective-permute-done.13
  237.7 5.3 collective-permute-start.14
  244.2 19.9 %collective-permute-done.14 = f32[4,40,2048]{2,1,0:T(8,128)S(1)} collective-permute-done((f32[4,40,2048]{2,1,0:T(8,128)S(1)}, f32[4,40,2048]{2,1,0:T(8,128)S(1)}, u32[]{:S(2)}, u32[]{:S(2)}) %collective-permute-start.14) | collective-permute-done | bytes 1310752 | tf_op jit(solution)/shard_map/ppermute | solution.py:28
  264.1 3.9 collective-permute-done.15
  268.1 3.1 fusion.61
  272.7 4.8 collective-permute-start.16
  282.6 15.1 %collective-permute-done.16 = f32[4,40,2048]{2,1,0:T(8,128)S(1)} collective-permute-done((f32[4,40,2048]{2,1,0:T(8,128)S(1)}, f32[4,40,2048]{2,1,0:T(8,128)S(1)}, u32[]{:S(2)}, u32[]{:S(2)}) %collective-permute-start.16) | collective-permute-done | bytes 1310752 | tf_op jit(solution)/shard_map/ppermute | solution.py:17
  299.1 4.2 collective-permute-done.17
  310.6 6.3 %copy.21 = f32[64,32,720]{2,1,0:T(8,128)} copy(f32[64,32,720]{2,0,1:T(8,128)S(1)} %fusion.67) | data formatting | bytes 11796480 | tf_op jit(solution)/shard_map/kb,bqc->kqc/dot_general | solution.py:107
  316.9 234.6 %reduce-scatter.2.cloned.1.call-done = f32[64,720]{1,0:T(8,128)} async-done(((f32[2048,720]{1,0:T(8,128)}), f32[64,720]{1,0:T(8,128)}) %reduce-scatter.2.cloned.1.call-update) | async-done | bytes 184336 | tf_op jit(solution)/shard_map/reduce_scatter | solution.py:106
  551.6 67.3 %all-reduce.2.cloned.1.call-done = f32[64,720]{1,0:T(8,128)} async-done(((f32[64,720]{1,0:T(8,128)}), f32[64,720]{1,0:T(8,128)}) %all-reduce.2.cloned.1.call-update) | async-done | bytes 184336 | tf_op jit(solution)/shard_map/psum | solution.py:112
  (65 shorter events, 56.4 us)
Async XLA Ops:
  6.5 300.2 %copy-start = (bf16[1,2048,720]{1,2,0:T(8,128)(2,1)S(1)}, bf16[1,2048,720]{1,2,0:T(8,128)(2,1)}, u32[]{:S(2)}) copy-start(bf16[1,2048,720]{1,2,0:T(8,128)(2,1)} %param.11) | copy-start | bytes 8847364
  6.5 10.4 %copy-start.5 = (s32[64]{0:T(128)S(1)}, s32[64]{0:T(128)}, u32[]{:S(2)}) copy-start(s32[64]{0:T(128)} %param.8) | copy-start | bytes 772
  6.5 10.5 %copy-start.3 = (f32[64,65]{1,0:T(8,128)S(1)}, f32[64,65]{1,0:T(8,128)}, u32[]{:S(2)}) copy-start(f32[64,65]{1,0:T(8,128)} %param.7) | copy-start | bytes 49924
  6.5 545.0 %reduce-scatter.2.cloned.1.call-start = ((), (), s32[]{:S(2)}) async-start(), calls=%async_computation.1 | async-start | bytes 6488064 | tf_op jit(solution)/shard_map/reduce_scatter | solution.py:106
  10.2 32.1 %collective-permute-start = (f32[4,40,2048]{2,1,0:T(8,128)}, f32[4,40,2048]{2,1,0:T(8,128)}, u32[]{:S(2)}, u32[]{:S(2)}) collective-permute-start(f32[4,40,2048]{2,1,0:T(8,128)} %get-tuple-element.13), channel_id=1, source_target_pairs={{0,1},{1,2},{2,3},{3,4},{4,5},{5,6},{6,7},{7,8},{8,9},{9,10},{10,1... | collective-permute-start | bytes 3932168 | tf_op jit(solution)/shard_map/ppermute | solution.py:28
  15.7 31.5 %collective-permute-start.1 = (f32[4,40,2048]{2,1,0:T(8,128)}, f32[4,40,2048]{2,1,0:T(8,128)}, u32[]{:S(2)}, u32[]{:S(2)}) collective-permute-start(f32[4,40,2048]{2,1,0:T(8,128)} %get-tuple-element.14), channel_id=1, source_target_pairs={{1,0},{2,1},{3,2},{4,3},{5,4},{6,5},{7,6},{8,7},{9,8},{10,9},{11,1... | collective-permute-start | bytes 3932168 | tf_op jit(solution)/shard_map/ppermute | solution.py:30
  54.9 39.0 %collective-permute-start.2 = (f32[4,40,2048]{2,1,0:T(8,128)S(1)}, f32[4,40,2048]{2,1,0:T(8,128)S(1)}, u32[]{:S(2)}, u32[]{:S(2)}) collective-permute-start(f32[4,40,2048]{2,1,0:T(8,128)S(1)} %convolution_bitcast_fusion.7), channel_id=1, source_target_pairs={{0,1},{1,2},{2,3},{3,4},{4,5},{5,6},{6,7},{7,8},{8,9},{9,10},{10,1... | collective-permute-start | bytes 3932168 | tf_op jit(solution)/shard_map/ppermute | solution.py:17
  59.5 35.8 %collective-permute-start.3 = (f32[4,40,2048]{2,1,0:T(8,128)S(1)}, f32[4,40,2048]{2,1,0:T(8,128)S(1)}, u32[]{:S(2)}, u32[]{:S(2)}) collective-permute-start(f32[4,40,2048]{2,1,0:T(8,128)S(1)} %convolution_bitcast_fusion.6), channel_id=1, source_target_pairs={{1,0},{2,1},{3,2},{4,3},{5,4},{6,5},{7,6},{8,7},{9,8},{10,9},{11,1... | collective-permute-start | bytes 3932168 | tf_op jit(solution)/shard_map/ppermute | solution.py:17
  60.9 30.6 %collective-permute-start.5 = (f32[1,40,1]{1,2,0:T(1,128)S(1)}, f32[1,40,1]{1,2,0:T(1,128)S(1)}, u32[]{:S(2)}, u32[]{:S(2)}) collective-permute-start(f32[1,40,1]{1,2,0:T(1,128)S(1)} %bitcast.192), channel_id=1, source_target_pairs={{1,0},{2,1},{3,2},{4,3},{5,4},{6,5},{7,6},{8,7},{9,8},{10,9},{11,1... | collective-permute-start | bytes 488 | tf_op jit(solution)/shard_map/ppermute | solution.py:17
  62.2 29.5 %collective-permute-start.4 = (f32[1,40,1]{1,2,0:T(1,128)S(1)}, f32[1,40,1]{1,2,0:T(1,128)S(1)}, u32[]{:S(2)}, u32[]{:S(2)}) collective-permute-start(f32[1,40,1]{1,2,0:T(1,128)S(1)} %bitcast.191), channel_id=1, source_target_pairs={{0,1},{1,2},{2,3},{3,4},{4,5},{5,6},{6,7},{7,8},{8,9},{9,10},{10,1... | collective-permute-start | bytes 488 | tf_op jit(solution)/shard_map/ppermute | solution.py:17
  93.9 1.6 copy-start.1
  97.5 29.1 %collective-permute-start.6 = (f32[4,40,2048]{2,1,0:T(8,128)S(1)}, f32[4,40,2048]{2,1,0:T(8,128)S(1)}, u32[]{:S(2)}, u32[]{:S(2)}) collective-permute-start(f32[4,40,2048]{2,1,0:T(8,128)S(1)} %get-tuple-element.11), channel_id=1, source_target_pairs={{0,1},{1,2},{2,3},{3,4},{4,5},{5,6},{6,7},{7,8},{8,9},{9,10},{10,1... | collective-permute-start | bytes 3932168 | tf_op jit(solution)/shard_map/ppermute | solution.py:28
  101.6 29.0 %collective-permute-start.7 = (f32[4,40,2048]{2,1,0:T(8,128)S(1)}, f32[4,40,2048]{2,1,0:T(8,128)S(1)}, u32[]{:S(2)}, u32[]{:S(2)}) collective-permute-start(f32[4,40,2048]{2,1,0:T(8,128)S(1)} %get-tuple-element.12), channel_id=1, source_target_pairs={{1,0},{2,1},{3,2},{4,3},{5,4},{6,5},{7,6},{8,7},{9,8},{10,9},{11,1... | collective-permute-start | bytes 3932168 | tf_op jit(solution)/shard_map/ppermute | solution.py:30
  135.3 26.6 %collective-permute-start.8 = (f32[4,40,2048]{2,1,0:T(8,128)S(1)}, f32[4,40,2048]{2,1,0:T(8,128)S(1)}, u32[]{:S(2)}, u32[]{:S(2)}) collective-permute-start(f32[4,40,2048]{2,1,0:T(8,128)S(1)} %convolution_bitcast_fusion.5), channel_id=1, source_target_pairs={{0,1},{1,2},{2,3},{3,4},{4,5},{5,6},{6,7},{7,8},{8,9},{9,10},{10,1... | collective-permute-start | bytes 3932168 | tf_op jit(solution)/shard_map/ppermute | solution.py:17
  139.7 27.9 %collective-permute-start.9 = (f32[4,40,2048]{2,1,0:T(8,128)S(1)}, f32[4,40,2048]{2,1,0:T(8,128)S(1)}, u32[]{:S(2)}, u32[]{:S(2)}) collective-permute-start(f32[4,40,2048]{2,1,0:T(8,128)S(1)} %convolution_bitcast_fusion.4), channel_id=1, source_target_pairs={{1,0},{2,1},{3,2},{4,3},{5,4},{6,5},{7,6},{8,7},{9,8},{10,9},{11,1... | collective-permute-start | bytes 3932168 | tf_op jit(solution)/shard_map/ppermute | solution.py:17
  169.6 26.4 %collective-permute-start.10 = (f32[4,40,2048]{2,1,0:T(8,128)S(1)}, f32[4,40,2048]{2,1,0:T(8,128)S(1)}, u32[]{:S(2)}, u32[]{:S(2)}) collective-permute-start(f32[4,40,2048]{2,1,0:T(8,128)S(1)} %get-tuple-element.9), channel_id=1, source_target_pairs={{0,1},{1,2},{2,3},{3,4},{4,5},{5,6},{6,7},{7,8},{8,9},{9,10},{10,1... | collective-permute-start | bytes 3932168 | tf_op jit(solution)/shard_map/ppermute | solution.py:28
  173.2 27.0 %collective-permute-start.11 = (f32[4,40,2048]{2,1,0:T(8,128)S(1)}, f32[4,40,2048]{2,1,0:T(8,128)S(1)}, u32[]{:S(2)}, u32[]{:S(2)}) collective-permute-start(f32[4,40,2048]{2,1,0:T(8,128)S(1)} %get-tuple-element.10), channel_id=1, source_target_pairs={{1,0},{2,1},{3,2},{4,3},{5,4},{6,5},{7,6},{8,7},{9,8},{10,9},{11,1... | collective-permute-start | bytes 3932168 | tf_op jit(solution)/shard_map/ppermute | solution.py:30
  204.9 25.3 %collective-permute-start.12 = (f32[4,40,2048]{2,1,0:T(8,128)S(1)}, f32[4,40,2048]{2,1,0:T(8,128)S(1)}, u32[]{:S(2)}, u32[]{:S(2)}) collective-permute-start(f32[4,40,2048]{2,1,0:T(8,128)S(1)} %convolution_bitcast_fusion.3), channel_id=1, source_target_pairs={{0,1},{1,2},{2,3},{3,4},{4,5},{5,6},{6,7},{7,8},{8,9},{9,10},{10,1... | collective-permute-start | bytes 3932168 | tf_op jit(solution)/shard_map/ppermute | solution.py:17
  210.0 25.7 %collective-permute-start.13 = (f32[4,40,2048]{2,1,0:T(8,128)S(1)}, f32[4,40,2048]{2,1,0:T(8,128)S(1)}, u32[]{:S(2)}, u32[]{:S(2)}) collective-permute-start(f32[4,40,2048]{2,1,0:T(8,128)S(1)} %convolution_bitcast_fusion.2), channel_id=1, source_target_pairs={{1,0},{2,1},{3,2},{4,3},{5,4},{6,5},{7,6},{8,7},{9,8},{10,9},{11,1... | collective-permute-start | bytes 3932168 | tf_op jit(solution)/shard_map/ppermute | solution.py:17
  237.7 26.5 %collective-permute-start.14 = (f32[4,40,2048]{2,1,0:T(8,128)S(1)}, f32[4,40,2048]{2,1,0:T(8,128)S(1)}, u32[]{:S(2)}, u32[]{:S(2)}) collective-permute-start(f32[4,40,2048]{2,1,0:T(8,128)S(1)} %get-tuple-element.7), channel_id=1, source_target_pairs={{0,1},{1,2},{2,3},{3,4},{4,5},{5,6},{6,7},{7,8},{8,9},{9,10},{10,1... | collective-permute-start | bytes 3932168 | tf_op jit(solution)/shard_map/ppermute | solution.py:28
  242.9 25.1 %collective-permute-start.15 = (f32[4,40,2048]{2,1,0:T(8,128)S(1)}, f32[4,40,2048]{2,1,0:T(8,128)S(1)}, u32[]{:S(2)}, u32[]{:S(2)}) collective-permute-start(f32[4,40,2048]{2,1,0:T(8,128)S(1)} %get-tuple-element.8), channel_id=1, source_target_pairs={{1,0},{2,1},{3,2},{4,3},{5,4},{6,5},{7,6},{8,7},{9,8},{10,9},{11,1... | collective-permute-start | bytes 3932168 | tf_op jit(solution)/shard_map/ppermute | solution.py:30
  272.7 25.0 %collective-permute-start.16 = (f32[4,40,2048]{2,1,0:T(8,128)S(1)}, f32[4,40,2048]{2,1,0:T(8,128)S(1)}, u32[]{:S(2)}, u32[]{:S(2)}) collective-permute-start(f32[4,40,2048]{2,1,0:T(8,128)S(1)} %convolution_bitcast_fusion.1), channel_id=1, source_target_pairs={{0,1},{1,2},{2,3},{3,4},{4,5},{5,6},{6,7},{7,8},{8,9},{9,10},{10,1... | collective-permute-start | bytes 3932168 | tf_op jit(solution)/shard_map/ppermute | solution.py:17
  279.1 24.2 %collective-permute-start.17 = (f32[4,40,2048]{2,1,0:T(8,128)S(1)}, f32[4,40,2048]{2,1,0:T(8,128)S(1)}, u32[]{:S(2)}, u32[]{:S(2)}) collective-permute-start(f32[4,40,2048]{2,1,0:T(8,128)S(1)} %convolution_bitcast_fusion), channel_id=1, source_target_pairs={{1,0},{2,1},{3,2},{4,3},{5,4},{6,5},{7,6},{8,7},{9,8},{10,9},{11,1... | collective-permute-start | bytes 3932168 | tf_op jit(solution)/shard_map/ppermute | solution.py:17
  299.0 5.9 copy-start.2
  306.8 1.0 copy-start.4
  316.9 302.0 %all-reduce.2.cloned.1.call-start = ((), (), s32[]{:S(2)}) async-start(), calls=%async_computation.2 | async-start | bytes 393216 | tf_op jit(solution)/shard_map/psum | solution.py:112
Sparse Core Ops, SparseCore 0:
  317.0 234.5 reduce-scatter.1
  554.0 64.8 all-reduce.1
where the time goes:
time: 635 us; the launch traced here: 628 us
  waiting for transfers between devices  493 us (78%)
  matrix products  56.2 us (9%)
  starting transfers between devices  51.4 us (8%)
  between operations  14.1 us (2%)
  local copies, waits for them, and re-layouts  12.8 us (2%)
    reduce_scatter x1, waiting for transfers between devices, body(): lax.psum_scatter(jnp.einsum('kb,bqc->kqc', onehot, blocks, precision=lax....  235 us
    ppermute x4, waiting for transfers between devices, extended(): lax.ppermute(tail, axis, [(i, (i + 1) % count) for i in range(ends)])  88.1 us
    ppermute x10, waiting for transfers between devices, shifted(): return lax.ppermute(block, axis, route)  85.7 us
    psum x1, waiting for transfers between devices, body(): binned = lax.psum(owned, 'frames')  67.3 us
    ppermute x10, starting transfers between devices, shifted(): return lax.ppermute(block, axis, route)  27.9 us
    ppermute x4, starting transfers between devices, extended(): lax.ppermute(tail, axis, [(i, (i + 1) % count) for i in range(ends)])  18.3 us
    ppermute x4, waiting for transfers between devices, extended(): lax.ppermute(head, axis, [((i + 1) % count, i) for i in range(ends)])  16.9 us
    dot_general x4, matrix products, body(): jnp.einsum('ij,fjc->fic', band_mat, padded, precision=lax.Precision.HIGHEST)  15.4 us
  transfers between devices with their start and end apart: 20, of which 17 were waited for; matrix products, arithmetic and copies ran while one was open for 4% of the time, Pallas kernels for 0%

commit v1 on v0

v1 whole, which is shorter than its diff:
```python
import functools

import jax
import jax.numpy as jnp
from jax import lax
from jax.experimental import pallas as pl
from jax.experimental.pallas import tpu as pltpu
from jax.sharding import PartitionSpec as P

NY, NZ, NX, NC = 4, 8, 4, 2
TILES, GROUPS = NY * NZ, NX * NC
ROWS, COLS, TILE = 2048, 2048, 64
F_DEV, BAND, SHIFT, ITERS = 4, 65, 8, 4
REACH = (BAND - 1) // 2 + SHIFT
CHI, QB, NB = 720, 32, 8
BLK = 128
FRONT = 48
PADDED = ROWS + 2 * BLK - BLK
KBLKS = ROWS // BLK
CHIP = 768

F32, BF16 = jnp.float32, jnp.bfloat16
MESH = pl.DeviceIdType.MESH
VMEM_LIMIT = 60 * 1024 * 1024

OTHERS = [(dy, dz) for dz in (4, -3, 3, -2, 2, -1, 1, 0) for dy in (2, 1, -1, 0) if (dy, dz) != (0, 0)]


def position():
    group = lax.axis_index("frames")
    tile = lax.axis_index("rows")
    return group, tile, tile // NZ, lax.rem(tile, NZ)


def other_tile(y, z, offset):
    return lax.rem(y + offset[0] + NY, NY) * NZ + lax.rem(z + offset[1] + NZ, NZ)


def greet(group, y, z):
    barrier = pltpu.get_barrier_semaphore()
    for offset in OTHERS:
        pl.semaphore_signal(barrier, inc=1, device_id={"rows": other_tile(y, z, offset)}, device_id_type=MESH)
    for step in range(1, GROUPS):
        pl.semaphore_signal(barrier, inc=1, device_id={"frames": lax.rem(group + step, GROUPS)}, device_id_type=MESH)
    return barrier, len(OTHERS) + GROUPS - 1


def lanes(shape):
    return lax.broadcasted_iota(jnp.int32, shape, len(shape) - 1)


def sublanes(shape):
    return lax.broadcasted_iota(jnp.int32, shape, len(shape) - 2)


def halves(value):
    high = value.astype(BF16)
    return high, (value - high.astype(F32)).astype(BF16)


def remote(src, dst, send_sem, recv_sem, device):
    return pltpu.make_async_remote_copy(
        src_ref=src, dst_ref=dst, send_sem=send_sem, recv_sem=recv_sem, device_id=device, device_id_type=MESH
    )


def transpose_kernel(obs, kern, shift, columns, bands, packed, taps, send_a, recv_a, send_b, recv_b, send_c, recv_c):
    group, tile, y, z = position()
    barrier, greeted = greet(group, y, z)
    per = TILE // GROUPS

    taps[...] = jnp.zeros_like(taps)
    taps[:, :BAND] = kern[pl.ds(pl.multiple_of(group * per, per), per), :]
    rows_of = sublanes((per, BLK))
    moves = jnp.zeros((per, BLK), jnp.int32)
    for r in range(per):
        moves = jnp.where(rows_of == r, shift[group * per + r] + SHIFT, moves)
    plain = taps[...]
    moved = jnp.zeros((per, BLK), F32)
    for s in range(2 * SHIFT + 1):
        moved = jnp.where(moves == s, pltpu.roll(plain, s, 1) if s else plain, moved)
    target = tile * TILE + group * per + rows_of + lanes((per, BLK)) - REACH
    moved = jnp.where((target >= 0) & (target < ROWS), moved, 0.0)
    bands[tile, group] = moved

    left = lanes((TILE, BLK)) < BLK // 2

    @pl.loop(0, COLS // BLK)
    def _(m):
        part = [obs[f, :, pl.ds(pl.multiple_of(m * BLK, BLK), BLK)] for f in range(F_DEV)]
        turned = [pltpu.roll(p, BLK // 2, 1) for p in part]
        for pair in range(2):
            a, b = 2 * pair, 2 * pair + 1
            packed[2 * m, :, pair * BLK : (pair + 1) * BLK] = jnp.where(left, part[a], turned[b])
            packed[2 * m + 1, :, pair * BLK : (pair + 1) * BLK] = jnp.where(left, turned[a], part[b])

    columns[tile] = packed[tile]
    pl.semaphore_wait(barrier, greeted)

    first, big, last = [], [], []
    for n, offset in enumerate(OTHERS):
        copy = remote(bands.at[tile, group], bands.at[tile, group], send_b.at[n], recv_b.at[n], {"rows": other_tile(y, z, offset)})
        copy.start()
        first.append(copy)
    for n, offset in enumerate(OTHERS):
        to = other_tile(y, z, offset)
        copy = remote(packed.at[to], columns.at[tile], send_a.at[n], recv_a.at[n], {"rows": to})
        copy.start()
        big.append(copy)
    for copy in first:
        copy.wait()
    for step in range(1, GROUPS):
        to = lax.rem(group + step, GROUPS)
        copy = remote(bands.at[:, group], bands.at[:, group], send_c.at[step - 1], recv_c.at[step - 1], {"frames": to})
        copy.start()
        last.append(copy)
    for copy in big + last:
        copy.wait()


def restore_kernel(obs, taps, out, wide, fwd, adj, est, est_hi, est_lo, rat_hi, rat_lo):
    wide[0:FRONT, :] = jnp.zeros((FRONT, BLK), F32)
    wide[FRONT + ROWS :, :] = jnp.zeros((PADDED - FRONT - ROWS, BLK), F32)
    wide[FRONT : FRONT + ROWS, :] = taps[...]
    for ref in (est_hi, est_lo, rat_hi, rat_lo):
        ref[0:FRONT, :] = jnp.zeros((FRONT, 2 * BLK), BF16)
        ref[FRONT + ROWS :, :] = jnp.zeros((PADDED - FRONT - ROWS, 2 * BLK), BF16)

    @pl.loop(0, KBLKS)
    def _(k):
        row = pl.multiple_of(k * BLK, BLK)
        mine = wide[pl.ds(row + FRONT, BLK), :]
        mine = jnp.concatenate([mine, jnp.zeros_like(mine)], axis=1)
        mine = pltpu.roll(mine, FRONT - REACH, 1, stride=1, stride_axis=0)
        high, low = halves(mine)
        fwd[k, 0:BLK, :] = high
        fwd[k, BLK:, :] = low
        near = wide[pl.ds(row, 2 * BLK), :]
        near = jnp.concatenate([near, jnp.zeros_like(near)], axis=1)
        near = pltpu.roll(near, 2 * BLK - (FRONT + REACH), 1, stride=1, stride_axis=0)[:, :BLK]
        near = near / jnp.sum(near, axis=0, keepdims=True)
        high, low = halves(jnp.transpose(near))
        adj[k, 0:BLK, :] = high
        adj[k, BLK:, :] = low
        start = obs[pl.ds(row, BLK), :]
        est[pl.ds(row, BLK), :] = start
        high, low = halves(start)
        est_hi[pl.ds(row + FRONT, BLK), :] = high
        est_lo[pl.ds(row + FRONT, BLK), :] = low

    def product(mat, k, row, hi, lo):
        both = jnp.dot(mat[k], hi[pl.ds(row, 2 * BLK), :], preferred_element_type=F32)
        rest = jnp.dot(mat[k, 0:BLK, :], lo[pl.ds(row, 2 * BLK), :], preferred_element_type=F32)
        return both[:BLK] + (both[BLK:] + rest)

    def forward():
        @pl.loop(0, KBLKS)
        def _(k):
            row = pl.multiple_of(k * BLK, BLK)
            ratio = obs[pl.ds(row, BLK), :] / product(fwd, k, row, est_hi, est_lo)
            high, low = halves(ratio)
            rat_hi[pl.ds(row + FRONT, BLK), :] = high
            rat_lo[pl.ds(row + FRONT, BLK), :] = low

    @pl.loop(0, ITERS - 1)
    def _(repeat):
        forward()

        @pl.loop(0, KBLKS)
        def _(k):
            row = pl.multiple_of(k * BLK, BLK)
            value = est[pl.ds(row, BLK), :] * product(adj, k, row, rat_hi, rat_lo)
            est[pl.ds(row, BLK), :] = value
            high, low = halves(value)
            est_hi[pl.ds(row + FRONT, BLK), :] = high
            est_lo[pl.ds(row + FRONT, BLK), :] = low

    forward()
    left = lanes((TILE // 2, BLK)) < BLK // 2

    @pl.loop(0, KBLKS)
    def _(k):
        row = pl.multiple_of(k * BLK, BLK)
        value = est[pl.ds(row, BLK), :] * product(adj, k, row, rat_hi, rat_lo)
        value = value[:, :BLK] + value[:, BLK:]
        value = value + pltpu.roll(value, BLK // 2, 1)
        for half in range(2):
            top = half * TILE
            out[2 * k + half] = jnp.where(left, value[top : top + TILE // 2], value[top + TILE // 2 : top + TILE])


def bin_kernel(
    parts, cyc, ids, chi_hbm, out, chi, got, summed, shared, from_core, mixed, from_x, named, around, placed, from_z, own, final,
    chi_sem, send_a, recv_a, send_c, recv_c, send_x, recv_x, send_y, recv_y, send_z, recv_z, send_g, recv_g,
):
    group, tile, y, z = position()
    x, core = group // NC, lax.rem(group, NC)
    load = pltpu.make_async_copy(chi_hbm.at[0], chi, chi_sem)
    load.start()
    barrier, greeted = greet(group, y, z)

    share = QB // GROUPS
    q = sublanes((NB * QB, NB * QB))
    wanted = ((q // share) % NB) * QB + (q // QB) * share + q % share
    order = (lanes((NB * QB, NB * QB)) == wanted).astype(BF16)
    turn = functools.partial(lax.dot_general, dimension_numbers=(((1,), (1,)), ((), ())), preferred_element_type=F32)
    high, low = halves(cyc[...])
    high, low = turn(order, high).astype(BF16), turn(order, low).astype(BF16)
    weights = jnp.concatenate([high, high, low], axis=1)
    got[tile] = parts[tile]
    pl.semaphore_wait(barrier, greeted)

    copies = []
    for n, offset in enumerate(OTHERS):
        to = other_tile(y, z, offset)
        copy = remote(parts.at[to], got.at[tile], send_a.at[n], recv_a.at[n], {"rows": to})
        copy.start()
        copies.append(copy)
    for copy in copies:
        copy.wait()

    left = lanes((TILE // 2, BLK)) < BLK // 2
    for m in range(COLS // BLK):
        a, b = got[2 * m], got[2 * m + 1]
        summed[0 : TILE // 2, m * BLK : (m + 1) * BLK] = jnp.where(left, a, pltpu.roll(b, BLK // 2, 1))
        summed[TILE // 2 :, m * BLK : (m + 1) * BLK] = jnp.where(left, pltpu.roll(a, BLK // 2, 1), b)
    load.wait()
    total = jnp.zeros((NB * QB, CHI), F32)
    step = COLS // 4
    for m in range(4):
        high, low = halves(summed[:, m * step : (m + 1) * step])
        part = jnp.dot(weights, jnp.concatenate([high, low, high], axis=0), preferred_element_type=F32).astype(BF16)
        total = total + jnp.dot(part, chi[m * step : (m + 1) * step, :], preferred_element_type=F32)
    for i in range(NX):
        for j in range(NC):
            top = (i * NC + j) * QB
            shared[j, i] = total[top : top + QB]

    swap = remote(shared.at[1 - core], from_core, send_c, recv_c, {"frames": x * NC + 1 - core})
    swap.start()
    swap.wait()
    mixed[...] = shared[core] + from_core[...]
    copies = []
    for n in range(1, NX):
        to = lax.rem(x + n, NX)
        copy = remote(mixed.at[to], from_x.at[n - 1], send_x.at[n - 1], recv_x.at[n - 1], {"frames": to * NC + core})
        copy.start()
        copies.append(copy)
    for copy in copies:
        copy.wait()
    value = mixed[x] + from_x[0] + from_x[1] + from_x[2]

    last = CHIP - BLK
    named[:, 0:last] = value[:, 0:last]
    lane, sub = lanes((QB, BLK)), sublanes((QB, BLK))
    label = jnp.zeros((QB, BLK), jnp.int32)
    for b in range(NB):
        label = jnp.where(sub // share == b, ids[0, b], label)
    tail = jnp.concatenate([value[:, last:], jnp.zeros((QB, CHIP - CHI), F32)], axis=1)
    named[:, last:] = jnp.where(lane == CHI - last, label.astype(F32), tail)
    around[y] = named[...]
    copies = []
    for n in range(1, NY):
        to = lax.rem(y + n, NY) * NZ + z
        copy = remote(named, around.at[y], send_y.at[n - 1], recv_y.at[n - 1], {"rows": to})
        copy.start()
        copies.append(copy)
    for copy in copies:
        copy.wait()

    every = around[...].reshape(NY * QB, CHIP)
    label = every[:, CHI : CHI + 1]
    rows_of, slot = sublanes((NY * QB, NZ * 2 * share)), lanes((NY * QB, NZ * 2 * share))
    owner_block = 2 * (y * NZ) + slot // share
    hit = (label == owner_block.astype(F32)) & (rows_of % share == slot % share)
    hit = hit.astype(BF16)
    high, low = halves(every)
    low2 = (every - high.astype(F32) - low.astype(F32)).astype(BF16)
    place = functools.partial(lax.dot_general, dimension_numbers=(((0,), (0,)), ((), ())), preferred_element_type=F32)
    put = place(jnp.concatenate([hit, hit, hit], axis=0), jnp.concatenate([high, low, low2], axis=0))
    for k in range(NZ):
        placed[k] = put[k * 2 * share : (k + 1) * 2 * share, :CHI]
    copies = []
    for n in range(1, NZ):
        to = lax.rem(z + n, NZ)
        copy = remote(placed.at[to], from_z.at[n - 1], send_z.at[n - 1], recv_z.at[n - 1], {"rows": y * NZ + to})
        copy.start()
        copies.append(copy)
    for copy in copies:
        copy.wait()
    value = placed[z]
    for n in range(NZ - 1):
        value = value + from_z[n]
    own[...] = value
    final[group] = value
    copies = []
    for n in range(1, GROUPS):
        copy = remote(own, final.at[group], send_g.at[n - 1], recv_g.at[n - 1], {"frames": lax.rem(group + n, GROUPS)})
        copy.start()
        copies.append(copy)
    for copy in copies:
        copy.wait()
    low_half = sublanes((2 * share, CHI)) < share
    for j in range(GROUPS // 2):
        a, b = final[2 * j], final[2 * j + 1]
        out[8 * j : 8 * j + 8, :] = jnp.where(low_half, a, pltpu.roll(b, share, 0))
        out[QB + 8 * j : QB + 8 * j + 8, :] = jnp.where(low_half, pltpu.roll(a, share, 0), b)


def body(observed, kernel, row_shift, cycle_map, cycle_blocks, chi_map):
    vmem = pl.BlockSpec(memory_space=pltpu.VMEM)
    smem = pl.BlockSpec(memory_space=pltpu.SMEM)
    dma = pltpu.SemaphoreType.DMA
    count = len(OTHERS)
    columns, bands = pl.pallas_call(
        transpose_kernel,
        name="transpose",
        out_shape=(
            jax.ShapeDtypeStruct((TILES, TILE, 2 * BLK), F32),
            jax.ShapeDtypeStruct((TILES, GROUPS, TILE // GROUPS, BLK), F32),
        ),
        in_specs=[vmem, vmem, smem],
        out_specs=(vmem, vmem),
        scratch_shapes=[
            pltpu.VMEM((TILES, TILE, 2 * BLK), F32),
            pltpu.VMEM((TILE // GROUPS, BLK), F32),
            dma((count,)), dma((count,)), dma((count,)), dma((count,)), dma((GROUPS - 1,)), dma((GROUPS - 1,)),
        ],
        compiler_params=pltpu.CompilerParams(collective_id=0, has_side_effects=True, vmem_limit_bytes=VMEM_LIMIT),
    )(observed, kernel, row_shift)

    parts = pl.pallas_call(
        restore_kernel,
        name="restore",
        out_shape=jax.ShapeDtypeStruct((TILES, TILE // 2, BLK), F32),
        in_specs=[vmem, vmem],
        out_specs=vmem,
        scratch_shapes=[
            pltpu.VMEM((PADDED, BLK), F32),
            pltpu.VMEM((KBLKS, 2 * BLK, 2 * BLK), BF16),
            pltpu.VMEM((KBLKS, 2 * BLK, 2 * BLK), BF16),
            pltpu.VMEM((ROWS, 2 * BLK), F32),
        ]
        + [pltpu.VMEM((PADDED, 2 * BLK), BF16)] * 4,
        compiler_params=pltpu.CompilerParams(vmem_limit_bytes=VMEM_LIMIT),
    )(columns.reshape(ROWS, 2 * BLK), bands.reshape(ROWS, BLK))

    return pl.pallas_call(
        bin_kernel,
        name="bin",
        out_shape=jax.ShapeDtypeStruct((TILE, CHI), F32),
        in_specs=[vmem, vmem, smem, pl.BlockSpec(memory_space=pl.ANY)],
        out_specs=vmem,
        scratch_shapes=[
            pltpu.VMEM((COLS, CHI), BF16),
            pltpu.VMEM((TILES, TILE // 2, BLK), F32),
            pltpu.VMEM((TILE, COLS), F32),
            pltpu.VMEM((NC, NX, QB, CHI), F32),
            pltpu.VMEM((NX, QB, CHI), F32),
            pltpu.VMEM((NX, QB, CHI), F32),
            pltpu.VMEM((NX - 1, QB, CHI), F32),
            pltpu.VMEM((QB, CHIP), F32),
            pltpu.VMEM((NY, QB, CHIP), F32),
            pltpu.VMEM((NZ, 8, CHI), F32),
            pltpu.VMEM((NZ - 1, 8, CHI), F32),
            pltpu.VMEM((8, CHI), F32),
            pltpu.VMEM((GROUPS, 8, CHI), F32),
            dma, dma((count,)), dma((count,)), dma, dma,
            dma((NX - 1,)), dma((NX - 1,)), dma((NY - 1,)), dma((NY - 1,)),
            dma((NZ - 1,)), dma((NZ - 1,)), dma((GROUPS - 1,)), dma((GROUPS - 1,)),
        ],
        compiler_params=pltpu.CompilerParams(collective_id=1, has_side_effects=True, vmem_limit_bytes=VMEM_LIMIT),
    )(parts, cycle_map, cycle_blocks, chi_map)


def solution(mesh):
    return jax.shard_map(
        body,
        mesh=mesh,
        in_specs=(
            P("frames", "rows", None),
            P("rows", None),
            P("rows"),
            P("rows", None),
            P("rows", None),
            P("rows", None, None),
        ),
        out_specs=P("rows", None),
        check_vma=False,
    )
```

time: 635 us -> 157 us (0.25); the launches traced: 628 us -> 157 us
  waiting for transfers between devices: 493 us -> 0 us
  Pallas kernels: 0 us -> 152 us
  matrix products: 56.2 us -> 0 us
  starting transfers between devices: 51.4 us -> 0 us
  between operations: 14.1 us -> 0.02 us
  local copies, waits for them, and re-layouts: 12.8 us -> 4.41 us
    reduce_scatter x1 -> x0, waiting for transfers between devices: 235 us -> none  [body(): lax.psum_scatter(jnp.einsum('kb,bqc->kqc', onehot, blocks, precision=lax....]
    ppermute x18 -> x0, waiting for transfers between devices: 191 us -> none  [the longest x4 88.1 us: extended(): lax.ppermute(tail, axis, [(i, (i + 1) % count) for i in range(ends)])]
    pallas_call x0 -> x3, Pallas kernels: none -> 152 us  [the longest x1 65 us: body(): pl.pallas_call(transpose_kernel, name='transpose', out_shape=(jax.ShapeDt...]
    psum x1 -> x0, waiting for transfers between devices: 67.3 us -> none  [body(): binned = lax.psum(owned, 'frames')]
    dot_general x30 -> x0, matrix products: 56.2 us -> none  [the longest x4 15.4 us: body(): jnp.einsum('ij,fjc->fic', band_mat, padded, precision=lax.Precision.HIGHEST)]
    ppermute x18 -> x0, starting transfers between devices: 51.3 us -> none  [the longest x10 27.9 us: shifted(): return lax.ppermute(block, axis, route)]
    dot_general x2 -> x0, local copies, waits for them, and re-layouts: 6.41 us -> none  [the longest x1 6.31 us: body(): jnp.einsum('kb,bqc->kqc', onehot, blocks, precision=lax.Precision.HIGHEST)]
  transfers between devices with their start and end apart: 20 -> 0, of which waited for: 17 -> 0; matrix products, arithmetic and copies ran while one was open for 4% -> 0% of each run, Pallas kernels for 0% -> 0%
where the time goes in v1:
time: 157 us
  Pallas kernels  152 us (97%)
  local copies, waits for them, and re-layouts  4.41 us (3%)
    pallas_call x1, Pallas kernels, body(): pl.pallas_call(transpose_kernel, name='transpose', out_shape=(jax.ShapeDt...  65 us
    pallas_call x1, Pallas kernels, body(): pl.pallas_call(bin_kernel, name='bin', out_shape=jax.ShapeDtypeStruct((TI...  49.5 us
    pallas_call x1, Pallas kernels, body(): pl.pallas_call(restore_kernel, name='restore', out_shape=jax.ShapeDtypeSt...  37.9 us
    unnamed x4, local copies, waits for them, and re-layouts  4.41 us

profile of v1, /device:TPU:1, one launch (start us, length us, event | category | flops | bytes accessed | tf_op | source)
XLA Modules:
  0.0 156.8 jit_solution(1716873713753187263)
XLA Ops:
  0.0 0.0 copy-start
  0.0 65.0 %transpose.1 = (f32[32,64,256]{2,1,0:T(8,128)}, f32[32,8,8,128]{3,2,1,0:T(8,128)}) custom-call(f32[4,64,2048]{2,1,0:T(8,128)} %obs.1, f32[64,65]{1,0:T(8,128)} %kern.1, s32[64]{0:T(128)} %shift.1), custom_call_target="tpu_custom_call" | custom-call | tf_op jit(solution)/shard_map/transpose/pallas_call | solution.py:315
  65.0 37.9 %restore.1.parts = f32[32,32,128]{2,1,0:T(8,128)} custom-call(f32[2048,256]{1,0:T(8,128)} %bitcast.2, f32[2048,128]{1,0:T(8,128)} %bitcast.3), custom_call_target="tpu_custom_call" | custom-call | tf_op jit(solution)/shard_map/restore/pallas_call | solution.py:332
  102.9 0.0 copy-done
  102.9 2.8 %copy.7.chi_hbm = bf16[1,2048,720]{2,1,0:T(8,128)(2,1)} copy(bf16[1,2048,720]{1,2,0:T(8,128)(2,1)S(1)} %copy-done) | data formatting | bytes 5898240 | tf_op args[5]
  105.7 49.5 %bin.1 = f32[64,720]{1,0:T(8,128)} custom-call(f32[32,32,128]{2,1,0:T(8,128)} %restore.1.parts, f32[64,256]{1,0:T(8,128)} %cyc.1, s32[1,8]{1,0:T(1,128)} %ids.1, bf16[1,2048,720]{2,1,0:T(8,128)(2,1)} %copy.7.chi_hbm), custom_call_target="tpu_custom_call" | custom-call | tf_op jit(solution)/shard_map/bin/pallas_call | solution.py:348
  155.2 1.6 %copy.9 = f32[64,720]{1,0:T(8,128)} copy(f32[64,720]{1,0:T(8,128)} %bin.1) | data formatting | bytes 368640
Async XLA Ops:
  0.0 102.9 %copy-start = (bf16[1,2048,720]{1,2,0:T(8,128)(2,1)S(1)}, bf16[1,2048,720]{1,2,0:T(8,128)(2,1)}, u32[]{:S(2)}) copy-start(bf16[1,2048,720]{1,2,0:T(8,128)(2,1)} %param.11) | copy-start | bytes 8847364

commit v2 on v1

--- a/solution.py
+++ b/solution.py
@@ -17,6 +17,7 @@
 FRONT = 48
 PADDED = ROWS + 2 * BLK - BLK
 KBLKS = ROWS // BLK
+GROUP = 4
 CHIP = 768
 
 F32, BF16 = jnp.float32, jnp.bfloat16
@@ -153,40 +154,56 @@
         rest = jnp.dot(mat[k, 0:BLK, :], lo[pl.ds(row, 2 * BLK), :], preferred_element_type=F32)
         return both[:BLK] + (both[BLK:] + rest)
 
-    def forward():
-        @pl.loop(0, KBLKS)
-        def _(k):
-            row = pl.multiple_of(k * BLK, BLK)
-            ratio = obs[pl.ds(row, BLK), :] / product(fwd, k, row, est_hi, est_lo)
-            high, low = halves(ratio)
-            rat_hi[pl.ds(row + FRONT, BLK), :] = high
-            rat_lo[pl.ds(row + FRONT, BLK), :] = low
+    def in_groups(step):
+        @pl.loop(0, KBLKS // GROUP)
+        def _(g):
+            blocks = []
+            for j in range(GROUP):
+                k = g * GROUP + j
+                row = pl.multiple_of(k * BLK, BLK)
+                blocks.append((row, step(row, k)))
+            for row, store in blocks:
+                store(row)
+
+    def store_halves(value, high_ref, low_ref, row):
+        high, low = halves(value)
+        high_ref[pl.ds(row + FRONT, BLK), :] = high
+        low_ref[pl.ds(row + FRONT, BLK), :] = low
+
+    def forward_block(row, k):
+        ratio = obs[pl.ds(row, BLK), :] / product(fwd, k, row, est_hi, est_lo)
+        return functools.partial(store_halves, ratio, rat_hi, rat_lo)
+
+    def adjoint_block(row, k):
+        value = est[pl.ds(row, BLK), :] * product(adj, k, row, rat_hi, rat_lo)
+
+        def store(row):
+            est[pl.ds(row, BLK), :] = value
+            store_halves(value, est_hi, est_lo, row)
+
+        return store
 
     @pl.loop(0, ITERS - 1)
     def _(repeat):
-        forward()
-
-        @pl.loop(0, KBLKS)
-        def _(k):
-            row = pl.multiple_of(k * BLK, BLK)
-            value = est[pl.ds(row, BLK), :] * product(adj, k, row, rat_hi, rat_lo)
-            est[pl.ds(row, BLK), :] = value
-            high, low = halves(value)
-            est_hi[pl.ds(row + FRONT, BLK), :] = high
-            est_lo[pl.ds(row + FRONT, BLK), :] = low
-
-    forward()
+        in_groups(forward_block)
+        in_groups(adjoint_block)
+
+    in_groups(forward_block)
     left = lanes((TILE // 2, BLK)) < BLK // 2
 
-    @pl.loop(0, KBLKS)
-    def _(k):
-        row = pl.multiple_of(k * BLK, BLK)
+    def last_block(row, k):
         value = est[pl.ds(row, BLK), :] * product(adj, k, row, rat_hi, rat_lo)
         value = value[:, :BLK] + value[:, BLK:]
         value = value + pltpu.roll(value, BLK // 2, 1)
-        for half in range(2):
-            top = half * TILE
-            out[2 * k + half] = jnp.where(left, value[top : top + TILE // 2], value[top + TILE // 2 : top + TILE])
+
+        def store(row):
+            for half in range(2):
+                top = half * TILE
+                out[2 * k + half] = jnp.where(left, value[top : top + TILE // 2], value[top + TILE // 2 : top + TILE])
+
+        return store
+
+    in_groups(last_block)
 
 
 def bin_kernel(
@@ -225,12 +242,13 @@
         summed[0 : TILE // 2, m * BLK : (m + 1) * BLK] = jnp.where(left, a, pltpu.roll(b, BLK // 2, 1))
         summed[TILE // 2 :, m * BLK : (m + 1) * BLK] = jnp.where(left, pltpu.roll(a, BLK // 2, 1), b)
     load.wait()
+    turn_chi = functools.partial(lax.dot_general, dimension_numbers=(((1,), (1,)), ((), ())), preferred_element_type=F32)
     total = jnp.zeros((NB * QB, CHI), F32)
     step = COLS // 4
     for m in range(4):
         high, low = halves(summed[:, m * step : (m + 1) * step])
         part = jnp.dot(weights, jnp.concatenate([high, low, high], axis=0), preferred_element_type=F32).astype(BF16)
-        total = total + jnp.dot(part, chi[m * step : (m + 1) * step, :], preferred_element_type=F32)
+        total = total + turn_chi(part, chi[:, m * step : (m + 1) * step])
     for i in range(NX):
         for j in range(NC):
             top = (i * NC + j) * QB
@@ -352,7 +370,7 @@
         in_specs=[vmem, vmem, smem, pl.BlockSpec(memory_space=pl.ANY)],
         out_specs=vmem,
         scratch_shapes=[
-            pltpu.VMEM((COLS, CHI), BF16),
+            pltpu.VMEM((CHI, COLS), BF16),
             pltpu.VMEM((TILES, TILE // 2, BLK), F32),
             pltpu.VMEM((TILE, COLS), F32),
             pltpu.VMEM((NC, NX, QB, CHI), F32),
@@ -370,7 +388,7 @@
             dma((NZ - 1,)), dma((NZ - 1,)), dma((GROUPS - 1,)), dma((GROUPS - 1,)),
         ],
         compiler_params=pltpu.CompilerParams(collective_id=1, has_side_effects=True, vmem_limit_bytes=VMEM_LIMIT),
-    )(parts, cycle_map, cycle_blocks, chi_map)
+    )(parts, cycle_map, cycle_blocks, jnp.swapaxes(chi_map, 1, 2))
 
 
 def solution(mesh):

time: 157 us -> 136 us (0.87)
  Pallas kernels: 152 us -> 134 us
  local copies, waits for them, and re-layouts: 4.41 us -> 1.62 us
    pallas_call x1, Pallas kernels: 37.9 us -> 19.5 us  [body(): pl.pallas_call(restore_kernel, name='restore', out_shape=jax.ShapeDtypeSt...]
    unnamed x4 -> x1, local copies, waits for them, and re-layouts: 4.41 us -> 1.62 us
where the time goes in v2:
time: 136 us; the launch traced here: 135 us
  Pallas kernels  134 us (99%)
  local copies, waits for them, and re-layouts  1.62 us (1%)
    pallas_call x1, Pallas kernels, body(): pl.pallas_call(transpose_kernel, name='transpose', out_shape=(jax.ShapeDt...  64.8 us
    pallas_call x1, Pallas kernels, body(): pl.pallas_call(bin_kernel, name='bin', out_shape=jax.ShapeDtypeStruct((TI...  49.5 us
    pallas_call x1, Pallas kernels, body(): pl.pallas_call(restore_kernel, name='restore', out_shape=jax.ShapeDtypeSt...  19.5 us

profile of v2, /device:TPU:1, one launch (start us, length us, event | category | flops | bytes accessed | tf_op | source)
XLA Modules:
  0.0 135.5 jit_solution(11058409518350332959)
XLA Ops:
  0.0 64.8 %transpose.5 = (f32[32,64,256]{2,1,0:T(8,128)}, f32[32,8,8,128]{3,2,1,0:T(8,128)}) custom-call(f32[4,64,2048]{2,1,0:T(8,128)} %obs.1, f32[64,65]{1,0:T(8,128)} %kern.1, s32[64]{0:T(128)} %shift.1), custom_call_target="tpu_custom_call" | custom-call | tf_op jit(solution)/shard_map/transpose/pallas_call | solution.py:333
  64.9 19.5 %restore.1.parts = f32[32,32,128]{2,1,0:T(8,128)} custom-call(f32[2048,256]{1,0:T(8,128)} %bitcast.4, f32[2048,128]{1,0:T(8,128)} %bitcast.5), custom_call_target="tpu_custom_call" | custom-call | tf_op jit(solution)/shard_map/restore/pallas_call | solution.py:350
  84.4 49.5 %bin.1 = f32[64,720]{1,0:T(8,128)} custom-call(f32[32,32,128]{2,1,0:T(8,128)} %restore.1.parts, f32[64,256]{1,0:T(8,128)} %cyc.1, s32[1,8]{1,0:T(1,128)} %ids.1, bf16[1,720,2048]{2,1,0:T(8,128)(2,1)} %bitcast.3), custom_call_target="tpu_custom_call" | custom-call | tf_op jit(solution)/shard_map/bin/pallas_call | solution.py:366
  133.8 1.6 %copy.8 = f32[64,720]{1,0:T(8,128)} copy(f32[64,720]{1,0:T(8,128)} %bin.1) | data formatting | bytes 368640

commit v3 on v2

--- a/solution.py
+++ b/solution.py
@@ -65,8 +65,16 @@
     )
 
 
-def transpose_kernel(obs, kern, shift, columns, bands, packed, taps, send_a, recv_a, send_b, recv_b, send_c, recv_c):
+def program_kernel(
+    obs, kern, shift, cyc, ids, chi_hbm, out, packed_0, packed_1, columns_0, columns_1, bands, taps, wide, fwd, adj, est, kept,
+    est_hl, rat_hl, weights, parts, chi, got, summed, shared, from_core, mixed, from_x, named, around, placed, from_z, own, final,
+    chi_sem, send_0, recv_0, send_1, recv_1, send_t, recv_t, send_f, recv_f,
+    send_a, recv_a, send_c, recv_c, send_x, recv_x, send_y, recv_y, send_z, recv_z, send_g, recv_g,
+):
     group, tile, y, z = position()
+    x, core = group // NC, lax.rem(group, NC)
+    load = pltpu.make_async_copy(chi_hbm.at[0], chi, chi_sem)
+    load.start()
     barrier, greeted = greet(group, y, z)
     per = TILE // GROUPS
 
@@ -84,48 +92,65 @@
     moved = jnp.where((target >= 0) & (target < ROWS), moved, 0.0)
     bands[tile, group] = moved
 
-    left = lanes((TILE, BLK)) < BLK // 2
-
-    @pl.loop(0, COLS // BLK)
-    def _(m):
-        part = [obs[f, :, pl.ds(pl.multiple_of(m * BLK, BLK), BLK)] for f in range(F_DEV)]
-        turned = [pltpu.roll(p, BLK // 2, 1) for p in part]
-        for pair in range(2):
-            a, b = 2 * pair, 2 * pair + 1
-            packed[2 * m, :, pair * BLK : (pair + 1) * BLK] = jnp.where(left, part[a], turned[b])
-            packed[2 * m + 1, :, pair * BLK : (pair + 1) * BLK] = jnp.where(left, turned[a], part[b])
-
-    columns[tile] = packed[tile]
+    def pack(pair, packed, columns):
+        left = lanes((TILE, BLK)) < BLK // 2
+
+        @pl.loop(0, COLS // BLK)
+        def _(m):
+            a, b = [obs[2 * pair + f, :, pl.ds(pl.multiple_of(m * BLK, BLK), BLK)] for f in range(2)]
+            packed[2 * m] = jnp.where(left, a, pltpu.roll(b, BLK // 2, 1))
+            packed[2 * m + 1] = jnp.where(left, pltpu.roll(a, BLK // 2, 1), b)
+
+        columns[tile] = packed[tile]
+
+    def exchange(packed, columns, send, recv):
+        started = []
+        for n, offset in enumerate(OTHERS):
+            to = other_tile(y, z, offset)
+            copy = remote(packed.at[to], columns.at[tile], send.at[n], recv.at[n], {"rows": to})
+            copy.start()
+            started.append(copy)
+        return started
+
+    pack(0, packed_0, columns_0)
     pl.semaphore_wait(barrier, greeted)
-
-    first, big, last = [], [], []
+    first = []
     for n, offset in enumerate(OTHERS):
-        copy = remote(bands.at[tile, group], bands.at[tile, group], send_b.at[n], recv_b.at[n], {"rows": other_tile(y, z, offset)})
+        copy = remote(bands.at[tile, group], bands.at[tile, group], send_t.at[n], recv_t.at[n], {"rows": other_tile(y, z, offset)})
         copy.start()
         first.append(copy)
-    for n, offset in enumerate(OTHERS):
-        to = other_tile(y, z, offset)
-        copy = remote(packed.at[to], columns.at[tile], send_a.at[n], recv_a.at[n], {"rows": to})
-        copy.start()
-        big.append(copy)
+    pair_0 = exchange(packed_0, columns_0, send_0, recv_0)
+    pack(1, packed_1, columns_1)
+    pair_1 = exchange(packed_1, columns_1, send_1, recv_1)
     for copy in first:
         copy.wait()
+    shares = []
     for step in range(1, GROUPS):
         to = lax.rem(group + step, GROUPS)
-        copy = remote(bands.at[:, group], bands.at[:, group], send_c.at[step - 1], recv_c.at[step - 1], {"frames": to})
-        copy.start()
-        last.append(copy)
-    for copy in big + last:
-        copy.wait()
-
-
-def restore_kernel(obs, taps, out, wide, fwd, adj, est, est_hi, est_lo, rat_hi, rat_lo):
+        copy = remote(bands.at[:, group], bands.at[:, group], send_f.at[step - 1], recv_f.at[step - 1], {"frames": to})
+        copy.start()
+        shares.append(copy)
+
+    share = QB // GROUPS
+    q = sublanes((NB * QB, NB * QB))
+    wanted = ((q // share) % NB) * QB + (q // QB) * share + q % share
+    order = (lanes((NB * QB, NB * QB)) == wanted).astype(BF16)
+    turn = functools.partial(lax.dot_general, dimension_numbers=(((1,), (1,)), ((), ())), preferred_element_type=F32)
+    high, low = halves(cyc[...])
+    high, low = turn(order, high).astype(BF16), turn(order, low).astype(BF16)
+    weights[...] = jnp.concatenate([high, high, low], axis=1)
+
+    for ref in (est_hl, rat_hl):
+        ref[0:FRONT, :] = jnp.zeros((FRONT, 2 * BLK), BF16)
+        ref[FRONT + ROWS :, :] = jnp.zeros((PADDED - FRONT - ROWS, 2 * BLK), BF16)
     wide[0:FRONT, :] = jnp.zeros((FRONT, BLK), F32)
     wide[FRONT + ROWS :, :] = jnp.zeros((PADDED - FRONT - ROWS, BLK), F32)
-    wide[FRONT : FRONT + ROWS, :] = taps[...]
-    for ref in (est_hi, est_lo, rat_hi, rat_lo):
-        ref[0:FRONT, :] = jnp.zeros((FRONT, 2 * BLK), BF16)
-        ref[FRONT + ROWS :, :] = jnp.zeros((PADDED - FRONT - ROWS, 2 * BLK), BF16)
+    for copy in shares:
+        copy.wait()
+
+    @pl.loop(0, TILES)
+    def _(t):
+        wide[pl.ds(pl.multiple_of(t * TILE, TILE) + FRONT, TILE), :] = bands[t].reshape(TILE, BLK)
 
     @pl.loop(0, KBLKS)
     def _(k):
@@ -143,16 +168,10 @@
         high, low = halves(jnp.transpose(near))
         adj[k, 0:BLK, :] = high
         adj[k, BLK:, :] = low
-        start = obs[pl.ds(row, BLK), :]
-        est[pl.ds(row, BLK), :] = start
-        high, low = halves(start)
-        est_hi[pl.ds(row + FRONT, BLK), :] = high
-        est_lo[pl.ds(row + FRONT, BLK), :] = low
-
-    def product(mat, k, row, hi, lo):
-        both = jnp.dot(mat[k], hi[pl.ds(row, 2 * BLK), :], preferred_element_type=F32)
-        rest = jnp.dot(mat[k, 0:BLK, :], lo[pl.ds(row, 2 * BLK), :], preferred_element_type=F32)
-        return both[:BLK] + (both[BLK:] + rest)
+
+    def product(mat, k, row, field):
+        both = jnp.dot(mat[k], field[pl.ds(row, 2 * BLK), :], preferred_element_type=F32)
+        return both[:BLK, :BLK] + (both[BLK:, :BLK] + both[:BLK, BLK:])
 
     def in_groups(step):
         @pl.loop(0, KBLKS // GROUP)
@@ -165,67 +184,75 @@
             for row, store in blocks:
                 store(row)
 
-    def store_halves(value, high_ref, low_ref, row):
+    def store_halves(value, field, row):
         high, low = halves(value)
-        high_ref[pl.ds(row + FRONT, BLK), :] = high
-        low_ref[pl.ds(row + FRONT, BLK), :] = low
-
-    def forward_block(row, k):
-        ratio = obs[pl.ds(row, BLK), :] / product(fwd, k, row, est_hi, est_lo)
-        return functools.partial(store_halves, ratio, rat_hi, rat_lo)
-
-    def adjoint_block(row, k):
-        value = est[pl.ds(row, BLK), :] * product(adj, k, row, rat_hi, rat_lo)
-
+        field[pl.ds(row + FRONT, BLK), 0:BLK] = high
+        field[pl.ds(row + FRONT, BLK), BLK:] = low
+
+    def restore(columns, last_block):
+        def seen(k):
+            return columns[pl.ds(2 * k, 2)].reshape(BLK, BLK)
+
+        def start_block(row, k):
+            value = seen(k)
+
+            def store(row):
+                est[pl.ds(row, BLK), :] = value
+                store_halves(value, est_hl, row)
+
+            return store
+
+        def forward_block(row, k):
+            return functools.partial(store_halves, seen(k) / product(fwd, k, row, est_hl), rat_hl)
+
+        def renewed(row, k):
+            return est[pl.ds(row, BLK), :] * product(adj, k, row, rat_hl)
+
+        def adjoint_block(row, k):
+            value = renewed(row, k)
+
+            def store(row):
+                est[pl.ds(row, BLK), :] = value
+                store_halves(value, est_hl, row)
+
+            return store
+
+        in_groups(start_block)
+
+        @pl.loop(0, ITERS - 1)
+        def _(repeat):
+            in_groups(forward_block)
+            in_groups(adjoint_block)
+
+        in_groups(forward_block)
+        in_groups(lambda row, k: last_block(row, k, renewed(row, k)))
+
+    left = lanes((TILE // 2, BLK)) < BLK // 2
+
+    def keep_block(row, k, value):
         def store(row):
-            est[pl.ds(row, BLK), :] = value
-            store_halves(value, est_hi, est_lo, row)
+            kept[pl.ds(row, BLK), :] = value
 
         return store
 
-    @pl.loop(0, ITERS - 1)
-    def _(repeat):
-        in_groups(forward_block)
-        in_groups(adjoint_block)
-
-    in_groups(forward_block)
-    left = lanes((TILE // 2, BLK)) < BLK // 2
-
-    def last_block(row, k):
-        value = est[pl.ds(row, BLK), :] * product(adj, k, row, rat_hi, rat_lo)
-        value = value[:, :BLK] + value[:, BLK:]
+    def sum_block(row, k, value):
+        value = kept[pl.ds(row, BLK), :] + value
         value = value + pltpu.roll(value, BLK // 2, 1)
 
         def store(row):
             for half in range(2):
                 top = half * TILE
-                out[2 * k + half] = jnp.where(left, value[top : top + TILE // 2], value[top + TILE // 2 : top + TILE])
+                parts[2 * k + half] = jnp.where(left, value[top : top + TILE // 2], value[top + TILE // 2 : top + TILE])
 
         return store
 
-    in_groups(last_block)
-
-
-def bin_kernel(
-    parts, cyc, ids, chi_hbm, out, chi, got, summed, shared, from_core, mixed, from_x, named, around, placed, from_z, own, final,
-    chi_sem, send_a, recv_a, send_c, recv_c, send_x, recv_x, send_y, recv_y, send_z, recv_z, send_g, recv_g,
-):
-    group, tile, y, z = position()
-    x, core = group // NC, lax.rem(group, NC)
-    load = pltpu.make_async_copy(chi_hbm.at[0], chi, chi_sem)
-    load.start()
-    barrier, greeted = greet(group, y, z)
-
-    share = QB // GROUPS
-    q = sublanes((NB * QB, NB * QB))
-    wanted = ((q // share) % NB) * QB + (q // QB) * share + q % share
-    order = (lanes((NB * QB, NB * QB)) == wanted).astype(BF16)
-    turn = functools.partial(lax.dot_general, dimension_numbers=(((1,), (1,)), ((), ())), preferred_element_type=F32)
-    high, low = halves(cyc[...])
-    high, low = turn(order, high).astype(BF16), turn(order, low).astype(BF16)
-    weights = jnp.concatenate([high, high, low], axis=1)
+    for copy in pair_0:
+        copy.wait()
+    restore(columns_0, keep_block)
+    for copy in pair_1:
+        copy.wait()
+    restore(columns_1, sum_block)
     got[tile] = parts[tile]
-    pl.semaphore_wait(barrier, greeted)
 
     copies = []
     for n, offset in enumerate(OTHERS):
@@ -236,7 +263,6 @@
     for copy in copies:
         copy.wait()
 
-    left = lanes((TILE // 2, BLK)) < BLK // 2
     for m in range(COLS // BLK):
         a, b = got[2 * m], got[2 * m + 1]
         summed[0 : TILE // 2, m * BLK : (m + 1) * BLK] = jnp.where(left, a, pltpu.roll(b, BLK // 2, 1))
@@ -247,7 +273,7 @@
     step = COLS // 4
     for m in range(4):
         high, low = halves(summed[:, m * step : (m + 1) * step])
-        part = jnp.dot(weights, jnp.concatenate([high, low, high], axis=0), preferred_element_type=F32).astype(BF16)
+        part = jnp.dot(weights[...], jnp.concatenate([high, low, high], axis=0), preferred_element_type=F32).astype(BF16)
         total = total + turn_chi(part, chi[:, m * step : (m + 1) * step])
     for i in range(NX):
         for j in range(NC):
@@ -330,46 +356,25 @@
     smem = pl.BlockSpec(memory_space=pltpu.SMEM)
     dma = pltpu.SemaphoreType.DMA
     count = len(OTHERS)
-    columns, bands = pl.pallas_call(
-        transpose_kernel,
-        name="transpose",
-        out_shape=(
-            jax.ShapeDtypeStruct((TILES, TILE, 2 * BLK), F32),
-            jax.ShapeDtypeStruct((TILES, GROUPS, TILE // GROUPS, BLK), F32),
-        ),
-        in_specs=[vmem, vmem, smem],
-        out_specs=(vmem, vmem),
-        scratch_shapes=[
-            pltpu.VMEM((TILES, TILE, 2 * BLK), F32),
+    return pl.pallas_call(
+        program_kernel,
+        name="restore_and_bin",
+        out_shape=jax.ShapeDtypeStruct((TILE, CHI), F32),
+        in_specs=[vmem, vmem, smem, vmem, smem, pl.BlockSpec(memory_space=pl.ANY)],
+        out_specs=vmem,
+        scratch_shapes=[pltpu.VMEM((TILES, TILE, BLK), F32)] * 4
+        + [
+            pltpu.VMEM((TILES, GROUPS, TILE // GROUPS, BLK), F32),
             pltpu.VMEM((TILE // GROUPS, BLK), F32),
-            dma((count,)), dma((count,)), dma((count,)), dma((count,)), dma((GROUPS - 1,)), dma((GROUPS - 1,)),
-        ],
-        compiler_params=pltpu.CompilerParams(collective_id=0, has_side_effects=True, vmem_limit_bytes=VMEM_LIMIT),
-    )(observed, kernel, row_shift)
-
-    parts = pl.pallas_call(
-        restore_kernel,
-        name="restore",
-        out_shape=jax.ShapeDtypeStruct((TILES, TILE // 2, BLK), F32),
-        in_specs=[vmem, vmem],
-        out_specs=vmem,
-        scratch_shapes=[
             pltpu.VMEM((PADDED, BLK), F32),
             pltpu.VMEM((KBLKS, 2 * BLK, 2 * BLK), BF16),
             pltpu.VMEM((KBLKS, 2 * BLK, 2 * BLK), BF16),
-            pltpu.VMEM((ROWS, 2 * BLK), F32),
-        ]
-        + [pltpu.VMEM((PADDED, 2 * BLK), BF16)] * 4,
-        compiler_params=pltpu.CompilerParams(vmem_limit_bytes=VMEM_LIMIT),
-    )(columns.reshape(ROWS, 2 * BLK), bands.reshape(ROWS, BLK))
-
-    return pl.pallas_call(
-        bin_kernel,
-        name="bin",
-        out_shape=jax.ShapeDtypeStruct((TILE, CHI), F32),
-        in_specs=[vmem, vmem, smem, pl.BlockSpec(memory_space=pl.ANY)],
-        out_specs=vmem,
-        scratch_shapes=[
+            pltpu.VMEM((ROWS, BLK), F32),
+            pltpu.VMEM((ROWS, BLK), F32),
+            pltpu.VMEM((PADDED, 2 * BLK), BF16),
+            pltpu.VMEM((PADDED, 2 * BLK), BF16),
+            pltpu.VMEM((NB * QB, 3 * TILE), BF16),
+            pltpu.VMEM((TILES, TILE // 2, BLK), F32),
             pltpu.VMEM((CHI, COLS), BF16),
             pltpu.VMEM((TILES, TILE // 2, BLK), F32),
             pltpu.VMEM((TILE, COLS), F32),
@@ -383,12 +388,15 @@
             pltpu.VMEM((NZ - 1, 8, CHI), F32),
             pltpu.VMEM((8, CHI), F32),
             pltpu.VMEM((GROUPS, 8, CHI), F32),
-            dma, dma((count,)), dma((count,)), dma, dma,
+            dma,
+            dma((count,)), dma((count,)), dma((count,)), dma((count,)),
+            dma((count,)), dma((count,)), dma((GROUPS - 1,)), dma((GROUPS - 1,)),
+            dma((count,)), dma((count,)), dma, dma,
             dma((NX - 1,)), dma((NX - 1,)), dma((NY - 1,)), dma((NY - 1,)),
             dma((NZ - 1,)), dma((NZ - 1,)), dma((GROUPS - 1,)), dma((GROUPS - 1,)),
         ],
-        compiler_params=pltpu.CompilerParams(collective_id=1, has_side_effects=True, vmem_limit_bytes=VMEM_LIMIT),
-    )(parts, cycle_map, cycle_blocks, jnp.swapaxes(chi_map, 1, 2))
+        compiler_params=pltpu.CompilerParams(collective_id=0, has_side_effects=True, vmem_limit_bytes=VMEM_LIMIT),
+    )(observed, kernel, row_shift, cycle_map, cycle_blocks, jnp.swapaxes(chi_map, 1, 2))
 
 
 def solution(mesh):

time: 136 us -> 121 us (0.89)
  Pallas kernels: 134 us -> 119 us
    pallas_call x3 -> x1, Pallas kernels: 134 us -> 119 us  [body(): pl.pallas_call(program_kernel, name='restore_and_bin', out_shape=jax.Shap...]
where the time goes in v3:
time: 121 us
  Pallas kernels  119 us (98%)
  local copies, waits for them, and re-layouts  1.62 us (1%)
    pallas_call x1, Pallas kernels, body(): pl.pallas_call(program_kernel, name='restore_and_bin', out_shape=jax.Shap...  119 us

profile of v3, /device:TPU:1, one launch (start us, length us, event | category | flops | bytes accessed | tf_op | source)
XLA Modules:
  0.0 120.7 jit_solution(2522252678698381033)
XLA Ops:
  0.0 119.1 %restore_and_bin.1 = f32[64,720]{1,0:T(8,128)} custom-call(f32[4,64,2048]{2,1,0:T(8,128)} %obs.1, f32[64,65]{1,0:T(8,128)} %kern.1, s32[64]{0:T(128)} %shift.1, f32[64,256]{1,0:T(8,128)} %cyc.1, s32[1,8]{1,0:T(1,128)} %ids.1, bf16[1,720,2048]{2,1,0:T(8,128)(2,1)} %bitcast.1), custom_call_target="tpu_custom_call" | custom-call | tf_op jit(solution)/shard_map/restore_and_bin/pallas_call | solution.py:359
  119.1 1.6 %copy.8 = f32[64,720]{1,0:T(8,128)} copy(f32[64,720]{1,0:T(8,128)} %restore_and_bin.1) | data formatting | bytes 368640

commit v4 on v3

--- a/solution.py
+++ b/solution.py
@@ -18,6 +18,7 @@
 PADDED = ROWS + 2 * BLK - BLK
 KBLKS = ROWS // BLK
 GROUP = 4
+PIECE = 32
 CHIP = 768
 
 F32, BF16 = jnp.float32, jnp.bfloat16
@@ -59,6 +60,14 @@
     return high, (value - high.astype(F32)).astype(BF16)
 
 
+def interleave(blocks, i, lane_group):
+    result = blocks[i]
+    for j in range(len(blocks)):
+        if j != i:
+            result = jnp.where(lane_group == j, pltpu.roll(blocks[j], PIECE * (j - i) % BLK, 1), result)
+    return result
+
+
 def remote(src, dst, send_sem, recv_sem, device):
     return pltpu.make_async_remote_copy(
         src_ref=src, dst_ref=dst, send_sem=send_sem, recv_sem=recv_sem, device_id=device, device_id_type=MESH
@@ -66,10 +75,10 @@
 
 
 def program_kernel(
-    obs, kern, shift, cyc, ids, chi_hbm, out, packed_0, packed_1, columns_0, columns_1, bands, taps, wide, fwd, adj, est, kept,
-    est_hl, rat_hl, weights, parts, chi, got, summed, shared, from_core, mixed, from_x, named, around, placed, from_z, own, final,
+    obs, kern, shift, cyc, ids, chi_hbm, out, packed_0, packed_1, columns_0, columns_1, bands, taps, wide, fwd, adj, est,
+    est_hl, rat_hl, weights, parts_0, parts_1, got_0, got_1, chi, summed, shared, from_core, mixed, from_x, named, around, placed, from_z, own, final,
     chi_sem, send_0, recv_0, send_1, recv_1, send_t, recv_t, send_f, recv_f,
-    send_a, recv_a, send_c, recv_c, send_x, recv_x, send_y, recv_y, send_z, recv_z, send_g, recv_g,
+    send_a, recv_a, send_b, recv_b, send_c, recv_c, send_x, recv_x, send_y, recv_y, send_z, recv_z, send_g, recv_g,
 ):
     group, tile, y, z = position()
     x, core = group // NC, lax.rem(group, NC)
@@ -92,14 +101,15 @@
     moved = jnp.where((target >= 0) & (target < ROWS), moved, 0.0)
     bands[tile, group] = moved
 
-    def pack(pair, packed, columns):
-        left = lanes((TILE, BLK)) < BLK // 2
-
-        @pl.loop(0, COLS // BLK)
+    lane_group = lanes((TILE, BLK)) // PIECE
+
+    def pack(half, packed, columns):
+        @pl.loop(0, COLS // BLK // 2)
         def _(m):
-            a, b = [obs[2 * pair + f, :, pl.ds(pl.multiple_of(m * BLK, BLK), BLK)] for f in range(2)]
-            packed[2 * m] = jnp.where(left, a, pltpu.roll(b, BLK // 2, 1))
-            packed[2 * m + 1] = jnp.where(left, pltpu.roll(a, BLK // 2, 1), b)
+            first_lane = pl.multiple_of((half * (COLS // BLK // 2) + m) * BLK, BLK)
+            frames = [obs[f, :, pl.ds(first_lane, BLK)] for f in range(F_DEV)]
+            for i in range(F_DEV):
+                packed[F_DEV * m + i] = interleave(frames, i, lane_group)
 
         columns[tile] = packed[tile]
 
@@ -119,9 +129,9 @@
         copy = remote(bands.at[tile, group], bands.at[tile, group], send_t.at[n], recv_t.at[n], {"rows": other_tile(y, z, offset)})
         copy.start()
         first.append(copy)
-    pair_0 = exchange(packed_0, columns_0, send_0, recv_0)
+    half_0 = exchange(packed_0, columns_0, send_0, recv_0)
     pack(1, packed_1, columns_1)
-    pair_1 = exchange(packed_1, columns_1, send_1, recv_1)
+    half_1 = exchange(packed_1, columns_1, send_1, recv_1)
     for copy in first:
         copy.wait()
     shares = []
@@ -227,54 +237,55 @@
         in_groups(forward_block)
         in_groups(lambda row, k: last_block(row, k, renewed(row, k)))
 
-    left = lanes((TILE // 2, BLK)) < BLK // 2
-
-    def keep_block(row, k, value):
-        def store(row):
-            kept[pl.ds(row, BLK), :] = value
-
-        return store
-
-    def sum_block(row, k, value):
-        value = kept[pl.ds(row, BLK), :] + value
-        value = value + pltpu.roll(value, BLK // 2, 1)
-
-        def store(row):
-            for half in range(2):
-                top = half * TILE
-                parts[2 * k + half] = jnp.where(left, value[top : top + TILE // 2], value[top + TILE // 2 : top + TILE])
-
-        return store
-
-    for copy in pair_0:
-        copy.wait()
-    restore(columns_0, keep_block)
-    for copy in pair_1:
-        copy.wait()
-    restore(columns_1, sum_block)
-    got[tile] = parts[tile]
-
-    copies = []
-    for n, offset in enumerate(OTHERS):
-        to = other_tile(y, z, offset)
-        copy = remote(parts.at[to], got.at[tile], send_a.at[n], recv_a.at[n], {"rows": to})
-        copy.start()
-        copies.append(copy)
-    for copy in copies:
-        copy.wait()
-
-    for m in range(COLS // BLK):
-        a, b = got[2 * m], got[2 * m + 1]
-        summed[0 : TILE // 2, m * BLK : (m + 1) * BLK] = jnp.where(left, a, pltpu.roll(b, BLK // 2, 1))
-        summed[TILE // 2 :, m * BLK : (m + 1) * BLK] = jnp.where(left, pltpu.roll(a, BLK // 2, 1), b)
+    quarter = TILE // F_DEV
+    quarter_group = lanes((quarter, BLK)) // PIECE
+
+    def sum_into(parts):
+        def sum_block(row, k, value):
+            value = value + pltpu.roll(value, BLK // 2, 1)
+            value = value + pltpu.roll(value, BLK // 4, 1)
+
+            def store(row):
+                for top in range(2):
+                    rows = [value[top * TILE + i * quarter : top * TILE + (i + 1) * quarter] for i in range(F_DEV)]
+                    result = rows[0]
+                    for i in range(1, F_DEV):
+                        result = jnp.where(quarter_group == i, rows[i], result)
+                    parts[2 * k + top] = result
+
+            return store
+
+        return sum_block
+
+    def bin_half(half, got, total):
+        for m in range(COLS // BLK // 2):
+            blocks = [got[F_DEV * m + j] for j in range(F_DEV)]
+            for i in range(F_DEV):
+                summed[i * quarter : (i + 1) * quarter, m * BLK : (m + 1) * BLK] = interleave(blocks, i, quarter_group)
+        step = COLS // 4
+        for m in range(2):
+            high, low = halves(summed[:, m * step : (m + 1) * step])
+            part = jnp.dot(weights[...], jnp.concatenate([high, low, high], axis=0), preferred_element_type=F32).astype(BF16)
+            total = total + turn(part, chi[:, (2 * half + m) * step : (2 * half + m + 1) * step])
+        return total
+
+    for copy in half_0:
+        copy.wait()
+    restore(columns_0, sum_into(parts_0))
+    got_0[tile] = parts_0[tile]
+    back_0 = exchange(parts_0, got_0, send_a, recv_a)
+    for copy in half_1:
+        copy.wait()
+    restore(columns_1, sum_into(parts_1))
+    got_1[tile] = parts_1[tile]
+    back_1 = exchange(parts_1, got_1, send_b, recv_b)
+    for copy in back_0:
+        copy.wait()
     load.wait()
-    turn_chi = functools.partial(lax.dot_general, dimension_numbers=(((1,), (1,)), ((), ())), preferred_element_type=F32)
-    total = jnp.zeros((NB * QB, CHI), F32)
-    step = COLS // 4
-    for m in range(4):
-        high, low = halves(summed[:, m * step : (m + 1) * step])
-        part = jnp.dot(weights[...], jnp.concatenate([high, low, high], axis=0), preferred_element_type=F32).astype(BF16)
-        total = total + turn_chi(part, chi[:, m * step : (m + 1) * step])
+    total = bin_half(0, got_0, jnp.zeros((NB * QB, CHI), F32))
+    for copy in back_1:
+        copy.wait()
+    total = bin_half(1, got_1, total)
     for i in range(NX):
         for j in range(NC):
             top = (i * NC + j) * QB
@@ -370,14 +381,14 @@
             pltpu.VMEM((KBLKS, 2 * BLK, 2 * BLK), BF16),
             pltpu.VMEM((KBLKS, 2 * BLK, 2 * BLK), BF16),
             pltpu.VMEM((ROWS, BLK), F32),
-            pltpu.VMEM((ROWS, BLK), F32),
             pltpu.VMEM((PADDED, 2 * BLK), BF16),
             pltpu.VMEM((PADDED, 2 * BLK), BF16),
             pltpu.VMEM((NB * QB, 3 * TILE), BF16),
-            pltpu.VMEM((TILES, TILE // 2, BLK), F32),
+        ]
+        + [pltpu.VMEM((TILES, TILE // F_DEV, BLK), F32)] * 4
+        + [
             pltpu.VMEM((CHI, COLS), BF16),
-            pltpu.VMEM((TILES, TILE // 2, BLK), F32),
-            pltpu.VMEM((TILE, COLS), F32),
+            pltpu.VMEM((TILE, COLS // 2), F32),
             pltpu.VMEM((NC, NX, QB, CHI), F32),
             pltpu.VMEM((NX, QB, CHI), F32),
             pltpu.VMEM((NX, QB, CHI), F32),
@@ -391,7 +402,7 @@
             dma,
             dma((count,)), dma((count,)), dma((count,)), dma((count,)),
             dma((count,)), dma((count,)), dma((GROUPS - 1,)), dma((GROUPS - 1,)),
-            dma((count,)), dma((count,)), dma, dma,
+            dma((count,)), dma((count,)), dma((count,)), dma((count,)), dma, dma,
             dma((NX - 1,)), dma((NX - 1,)), dma((NY - 1,)), dma((NY - 1,)),
             dma((NZ - 1,)), dma((NZ - 1,)), dma((GROUPS - 1,)), dma((GROUPS - 1,)),
         ],

time: 121 us -> 116 us (0.959)
  Pallas kernels: 119 us -> 114 us
    pallas_call x1, Pallas kernels: 119 us -> 114 us  [body(): pl.pallas_call(program_kernel, name='restore_and_bin', out_shape=jax.Shap...]
where the time goes in v4:
time: 116 us
  Pallas kernels  114 us (98%)
  local copies, waits for them, and re-layouts  1.62 us (1%)
    pallas_call x1, Pallas kernels, body(): pl.pallas_call(program_kernel, name='restore_and_bin', out_shape=jax.Shap...  114 us

profile of v4, /device:TPU:1, one launch (start us, length us, event | category | flops | bytes accessed | tf_op | source)
XLA Modules:
  0.0 115.7 jit_solution(18375234681443574315)
XLA Ops:
  0.0 114.1 %restore_and_bin.1 = f32[64,720]{1,0:T(8,128)} custom-call(f32[4,64,2048]{2,1,0:T(8,128)} %obs.1, f32[64,65]{1,0:T(8,128)} %kern.1, s32[64]{0:T(128)} %shift.1, f32[64,256]{1,0:T(8,128)} %cyc.1, s32[1,8]{1,0:T(1,128)} %ids.1, bf16[1,720,2048]{2,1,0:T(8,128)(2,1)} %bitcast.1), custom_call_target="tpu_custom_call" | custom-call | tf_op jit(solution)/shard_map/restore_and_bin/pallas_call | solution.py:370
  114.1 1.6 %copy.8 = f32[64,720]{1,0:T(8,128)} copy(f32[64,720]{1,0:T(8,128)} %restore_and_bin.1) | data formatting | bytes 368640

commit v5 on v4

--- a/solution.py
+++ b/solution.py
@@ -19,7 +19,7 @@
 KBLKS = ROWS // BLK
 GROUP = 4
 PIECE = 32
-CHIP = 768
+BINS = ((0, 384), (384, CHI))
 
 F32, BF16 = jnp.float32, jnp.bfloat16
 MESH = pl.DeviceIdType.MESH
@@ -76,10 +76,13 @@
 
 def program_kernel(
     obs, kern, shift, cyc, ids, chi_hbm, out, packed_0, packed_1, columns_0, columns_1, bands, taps, wide, fwd, adj, est,
-    est_hl, rat_hl, weights, parts_0, parts_1, got_0, got_1, chi, summed, shared, from_core, mixed, from_x, named, around, placed, from_z, own, final,
-    chi_sem, send_0, recv_0, send_1, recv_1, send_t, recv_t, send_f, recv_f,
-    send_a, recv_a, send_b, recv_b, send_c, recv_c, send_x, recv_x, send_y, recv_y, send_z, recv_z, send_g, recv_g,
+    est_hl, rat_hl, weights, parts_0, parts_1, got_0, got_1, chi, summed, cycles, labels, hits, *rest,
 ):
+    chunks, sems = rest[: 9 * len(BINS)], rest[9 * len(BINS) :]
+    (
+        chi_sem, send_0, recv_0, send_1, recv_1, send_t, recv_t, send_f, recv_f, send_l, recv_l, send_a, recv_a, send_b, recv_b,
+        send_c, recv_c, send_x, recv_x, send_y, recv_y, send_z, recv_z, send_g, recv_g,
+    ) = sems
     group, tile, y, z = position()
     x, core = group // NC, lax.rem(group, NC)
     load = pltpu.make_async_copy(chi_hbm.at[0], chi, chi_sem)
@@ -122,6 +125,13 @@
             started.append(copy)
         return started
 
+    share = QB // GROUPS
+    sub = sublanes((QB, BLK))
+    label = jnp.zeros((QB, BLK), jnp.int32)
+    for b in range(NB):
+        label = jnp.where(sub // share == b, ids[0, b], label)
+    labels[y] = label.astype(F32)
+
     pack(0, packed_0, columns_0)
     pl.semaphore_wait(barrier, greeted)
     first = []
@@ -129,6 +139,11 @@
         copy = remote(bands.at[tile, group], bands.at[tile, group], send_t.at[n], recv_t.at[n], {"rows": other_tile(y, z, offset)})
         copy.start()
         first.append(copy)
+    for n in range(1, NY):
+        to = lax.rem(y + n, NY) * NZ + z
+        copy = remote(labels.at[y], labels.at[y], send_l.at[n - 1], recv_l.at[n - 1], {"rows": to})
+        copy.start()
+        first.append(copy)
     half_0 = exchange(packed_0, columns_0, send_0, recv_0)
     pack(1, packed_1, columns_1)
     half_1 = exchange(packed_1, columns_1, send_1, recv_1)
@@ -141,7 +156,6 @@
         copy.start()
         shares.append(copy)
 
-    share = QB // GROUPS
     q = sublanes((NB * QB, NB * QB))
     wanted = ((q // share) % NB) * QB + (q // QB) * share + q % share
     order = (lanes((NB * QB, NB * QB)) == wanted).astype(BF16)
@@ -149,6 +163,11 @@
     high, low = halves(cyc[...])
     high, low = turn(order, high).astype(BF16), turn(order, low).astype(BF16)
     weights[...] = jnp.concatenate([high, high, low], axis=1)
+
+    rows_of, slot = sublanes((NY * QB, BLK)), lanes((NY * QB, BLK))
+    owner_block = 2 * (y * NZ) + slot // share
+    hit = (labels[...].reshape(NY * QB, BLK) == owner_block.astype(F32)) & (rows_of % share == slot % share)
+    hits[...] = hit.astype(BF16)[:, : NZ * 2 * share]
 
     for ref in (est_hl, rat_hl):
         ref[0:FRONT, :] = jnp.zeros((FRONT, 2 * BLK), BF16)
@@ -257,7 +276,7 @@
 
         return sum_block
 
-    def bin_half(half, got, total):
+    def cycle_parts(got):
         for m in range(COLS // BLK // 2):
             blocks = [got[F_DEV * m + j] for j in range(F_DEV)]
             for i in range(F_DEV):
@@ -265,8 +284,14 @@
         step = COLS // 4
         for m in range(2):
             high, low = halves(summed[:, m * step : (m + 1) * step])
-            part = jnp.dot(weights[...], jnp.concatenate([high, low, high], axis=0), preferred_element_type=F32).astype(BF16)
-            total = total + turn(part, chi[:, (2 * half + m) * step : (2 * half + m + 1) * step])
+            part = jnp.dot(weights[...], jnp.concatenate([high, low, high], axis=0), preferred_element_type=F32)
+            cycles[:, m * step : (m + 1) * step] = part.astype(BF16)
+
+    def add_bins(half, bins, total):
+        step = COLS // 4
+        for m in range(2):
+            place = (2 * half + m) * step
+            total = total + turn(cycles[:, m * step : (m + 1) * step], chi[bins[0] : bins[1], place : place + step])
         return total
 
     for copy in half_0:
@@ -282,84 +307,84 @@
     for copy in back_0:
         copy.wait()
     load.wait()
-    total = bin_half(0, got_0, jnp.zeros((NB * QB, CHI), F32))
+    cycle_parts(got_0)
+    totals = [add_bins(0, bins, jnp.zeros((NB * QB, bins[1] - bins[0]), F32)) for bins in BINS]
     for copy in back_1:
         copy.wait()
-    total = bin_half(1, got_1, total)
-    for i in range(NX):
-        for j in range(NC):
-            top = (i * NC + j) * QB
-            shared[j, i] = total[top : top + QB]
-
-    swap = remote(shared.at[1 - core], from_core, send_c, recv_c, {"frames": x * NC + 1 - core})
-    swap.start()
-    swap.wait()
-    mixed[...] = shared[core] + from_core[...]
-    copies = []
-    for n in range(1, NX):
-        to = lax.rem(x + n, NX)
-        copy = remote(mixed.at[to], from_x.at[n - 1], send_x.at[n - 1], recv_x.at[n - 1], {"frames": to * NC + core})
-        copy.start()
-        copies.append(copy)
-    for copy in copies:
-        copy.wait()
-    value = mixed[x] + from_x[0] + from_x[1] + from_x[2]
-
-    last = CHIP - BLK
-    named[:, 0:last] = value[:, 0:last]
-    lane, sub = lanes((QB, BLK)), sublanes((QB, BLK))
-    label = jnp.zeros((QB, BLK), jnp.int32)
-    for b in range(NB):
-        label = jnp.where(sub // share == b, ids[0, b], label)
-    tail = jnp.concatenate([value[:, last:], jnp.zeros((QB, CHIP - CHI), F32)], axis=1)
-    named[:, last:] = jnp.where(lane == CHI - last, label.astype(F32), tail)
-    around[y] = named[...]
-    copies = []
-    for n in range(1, NY):
-        to = lax.rem(y + n, NY) * NZ + z
-        copy = remote(named, around.at[y], send_y.at[n - 1], recv_y.at[n - 1], {"rows": to})
-        copy.start()
-        copies.append(copy)
-    for copy in copies:
-        copy.wait()
-
-    every = around[...].reshape(NY * QB, CHIP)
-    label = every[:, CHI : CHI + 1]
-    rows_of, slot = sublanes((NY * QB, NZ * 2 * share)), lanes((NY * QB, NZ * 2 * share))
-    owner_block = 2 * (y * NZ) + slot // share
-    hit = (label == owner_block.astype(F32)) & (rows_of % share == slot % share)
-    hit = hit.astype(BF16)
-    high, low = halves(every)
-    low2 = (every - high.astype(F32) - low.astype(F32)).astype(BF16)
-    place = functools.partial(lax.dot_general, dimension_numbers=(((0,), (0,)), ((), ())), preferred_element_type=F32)
-    put = place(jnp.concatenate([hit, hit, hit], axis=0), jnp.concatenate([high, low, low2], axis=0))
-    for k in range(NZ):
-        placed[k] = put[k * 2 * share : (k + 1) * 2 * share, :CHI]
-    copies = []
-    for n in range(1, NZ):
-        to = lax.rem(z + n, NZ)
-        copy = remote(placed.at[to], from_z.at[n - 1], send_z.at[n - 1], recv_z.at[n - 1], {"rows": y * NZ + to})
-        copy.start()
-        copies.append(copy)
-    for copy in copies:
-        copy.wait()
-    value = placed[z]
-    for n in range(NZ - 1):
-        value = value + from_z[n]
-    own[...] = value
-    final[group] = value
-    copies = []
-    for n in range(1, GROUPS):
-        copy = remote(own, final.at[group], send_g.at[n - 1], recv_g.at[n - 1], {"frames": lax.rem(group + n, GROUPS)})
-        copy.start()
-        copies.append(copy)
-    for copy in copies:
-        copy.wait()
-    low_half = sublanes((2 * share, CHI)) < share
-    for j in range(GROUPS // 2):
-        a, b = final[2 * j], final[2 * j + 1]
-        out[8 * j : 8 * j + 8, :] = jnp.where(low_half, a, pltpu.roll(b, share, 0))
-        out[QB + 8 * j : QB + 8 * j + 8, :] = jnp.where(low_half, pltpu.roll(a, share, 0), b)
+    cycle_parts(got_1)
+
+    def reduce_bins(c):
+        shared, from_core, mixed, from_x, around, placed, from_z, own, final = chunks[c :: len(BINS)]
+        bins = BINS[c]
+        total = add_bins(1, bins, totals[c])
+        for i in range(NX):
+            for j in range(NC):
+                top = (i * NC + j) * QB
+                shared[j, i] = total[top : top + QB]
+
+        swap = remote(shared.at[1 - core], from_core, send_c.at[c], recv_c.at[c], {"frames": x * NC + 1 - core})
+        swap.start()
+        yield
+        swap.wait()
+        mixed[...] = shared[core] + from_core[...]
+        copies = []
+        for n in range(1, NX):
+            to = lax.rem(x + n, NX)
+            copy = remote(mixed.at[to], from_x.at[n - 1], send_x.at[c, n - 1], recv_x.at[c, n - 1], {"frames": to * NC + core})
+            copy.start()
+            copies.append(copy)
+        yield
+        for copy in copies:
+            copy.wait()
+        around[y] = mixed[x] + from_x[0] + from_x[1] + from_x[2]
+        copies = []
+        for n in range(1, NY):
+            to = lax.rem(y + n, NY) * NZ + z
+            copy = remote(around.at[y], around.at[y], send_y.at[c, n - 1], recv_y.at[c, n - 1], {"rows": to})
+            copy.start()
+            copies.append(copy)
+        yield
+        for copy in copies:
+            copy.wait()
+        every = around[...].reshape(NY * QB, bins[1] - bins[0])
+        high, low = halves(every)
+        low2 = (every - high.astype(F32) - low.astype(F32)).astype(BF16)
+        place = functools.partial(lax.dot_general, dimension_numbers=(((0,), (0,)), ((), ())), preferred_element_type=F32)
+        put = place(jnp.concatenate([hits[...]] * 3, axis=0), jnp.concatenate([high, low, low2], axis=0))
+        for k in range(NZ):
+            placed[k] = put[k * 2 * share : (k + 1) * 2 * share]
+        copies = []
+        for n in range(1, NZ):
+            to = lax.rem(z + n, NZ)
+            copy = remote(placed.at[to], from_z.at[n - 1], send_z.at[c, n - 1], recv_z.at[c, n - 1], {"rows": y * NZ + to})
+            copy.start()
+            copies.append(copy)
+        yield
+        for copy in copies:
+            copy.wait()
+        value = placed[z]
+        for n in range(NZ - 1):
+            value = value + from_z[n]
+        own[...] = value
+        final[group] = value
+        copies = []
+        for n in range(1, GROUPS):
+            to = lax.rem(group + n, GROUPS)
+            copy = remote(own, final.at[group], send_g.at[c, n - 1], recv_g.at[c, n - 1], {"frames": to})
+            copy.start()
+            copies.append(copy)
+        yield
+        for copy in copies:
+            copy.wait()
+        low_half = sublanes((2 * share, bins[1] - bins[0])) < share
+        for j in range(GROUPS // 2):
+            a, b = final[2 * j], final[2 * j + 1]
+            out[8 * j : 8 * j + 8, bins[0] : bins[1]] = jnp.where(low_half, a, pltpu.roll(b, share, 0))
+            out[QB + 8 * j : QB + 8 * j + 8, bins[0] : bins[1]] = jnp.where(low_half, pltpu.roll(a, share, 0), b)
+
+    running = [reduce_bins(c) for c in range(len(BINS))]
+    while running:
+        running = [chunk for chunk in running if next(chunk, True) is None]
 
 
 def body(observed, kernel, row_shift, cycle_map, cycle_blocks, chi_map):
@@ -389,23 +414,20 @@
         + [
             pltpu.VMEM((CHI, COLS), BF16),
             pltpu.VMEM((TILE, COLS // 2), F32),
-            pltpu.VMEM((NC, NX, QB, CHI), F32),
-            pltpu.VMEM((NX, QB, CHI), F32),
-            pltpu.VMEM((NX, QB, CHI), F32),
-            pltpu.VMEM((NX - 1, QB, CHI), F32),
-            pltpu.VMEM((QB, CHIP), F32),
-            pltpu.VMEM((NY, QB, CHIP), F32),
-            pltpu.VMEM((NZ, 8, CHI), F32),
-            pltpu.VMEM((NZ - 1, 8, CHI), F32),
-            pltpu.VMEM((8, CHI), F32),
-            pltpu.VMEM((GROUPS, 8, CHI), F32),
-            dma,
-            dma((count,)), dma((count,)), dma((count,)), dma((count,)),
-            dma((count,)), dma((count,)), dma((GROUPS - 1,)), dma((GROUPS - 1,)),
-            dma((count,)), dma((count,)), dma((count,)), dma((count,)), dma, dma,
-            dma((NX - 1,)), dma((NX - 1,)), dma((NY - 1,)), dma((NY - 1,)),
-            dma((NZ - 1,)), dma((NZ - 1,)), dma((GROUPS - 1,)), dma((GROUPS - 1,)),
-        ],
+            pltpu.VMEM((NB * QB, COLS // 2), BF16),
+            pltpu.VMEM((NY, QB, BLK), F32),
+            pltpu.VMEM((NY * QB, NZ * 2 * QB // GROUPS), BF16),
+        ]
+        + [
+            pltpu.VMEM((*rows, last - start), F32)
+            for rows in (
+                (NC, NX, QB), (NX, QB), (NX, QB), (NX - 1, QB), (NY, QB), (NZ, 8), (NZ - 1, 8), (8,), (GROUPS, 8),
+            )
+            for start, last in BINS
+        ]
+        + [dma]
+        + [dma((n,)) for n in (count, count, count, GROUPS - 1, NY - 1, count, count, len(BINS)) for _ in range(2)]
+        + [dma((len(BINS), n)) for n in (NX - 1, NY - 1, NZ - 1, GROUPS - 1) for _ in range(2)],
         compiler_params=pltpu.CompilerParams(collective_id=0, has_side_effects=True, vmem_limit_bytes=VMEM_LIMIT),
     )(observed, kernel, row_shift, cycle_map, cycle_blocks, jnp.swapaxes(chi_map, 1, 2))
 

time: 116 us -> 112 us (0.966)
  Pallas kernels: 114 us -> 111 us
    pallas_call x1, Pallas kernels: 114 us -> 111 us  [body(): pl.pallas_call(program_kernel, name='restore_and_bin', out_shape=jax.Shap...]
where the time goes in v5:
time: 112 us
  Pallas kernels  111 us (99%)
  local copies, waits for them, and re-layouts  1.62 us (1%)
    pallas_call x1, Pallas kernels, body(): pl.pallas_call(program_kernel, name='restore_and_bin', out_shape=jax.Shap...  111 us

profile of v5, /device:TPU:1, one launch (start us, length us, event | category | flops | bytes accessed | tf_op | source)
XLA Modules:
  0.0 112.2 jit_solution(11574883912011456063)
XLA Ops:
  0.0 110.5 %restore_and_bin.1 = f32[64,720]{1,0:T(8,128)} custom-call(f32[4,64,2048]{2,1,0:T(8,128)} %obs.1, f32[64,65]{1,0:T(8,128)} %kern.1, s32[64]{0:T(128)} %shift.1, f32[64,256]{1,0:T(8,128)} %cyc.1, s32[1,8]{1,0:T(1,128)} %ids.1, bf16[1,720,2048]{2,1,0:T(8,128)(2,1)} %bitcast.1), custom_call_target="tpu_custom_call" | custom-call | tf_op jit(solution)/shard_map/restore_and_bin/pallas_call | solution.py:395
  110.5 1.6 %copy.8 = f32[64,720]{1,0:T(8,128)} copy(f32[64,720]{1,0:T(8,128)} %restore_and_bin.1) | data formatting | bytes 368640
